TPU v7x, 128 devices: a whole 4x4x4 slice. The times are simulated.
128 devices in a mesh: sec: 4 (over y), bulk: 32 (over x, z, core).
Axes of the slice: x: 4, y: 4, z: 4, core: 2. Of those that a mesh axis runs over, the one named last changes fastest.
Arguments:
- displacement: float32 [3, 16384], P(None, ('sec', 'bulk')), may hold values from -6 to 6
- nodal_load: float32 [3, 16384], P(None, ('sec', 'bulk')), may hold values from -12 to 12
- connectivity: int32 [4, 65536], P(None, ('sec', 'bulk')), may hold values from 0 to 127
- shape_grads: float32 [12, 65536], P(None, ('sec', 'bulk'))
- elem_volume: float32 [65536], P(('sec', 'bulk')), may hold values from 0.3 to 3
- point_map: int32 [65536], P(('sec', 'bulk')), may hold values from 0 to 65535, as said below
- vol_blocks: int32 [32, 8], P('bulk'), may hold values from 1 to 4, as said below
- c_affine: float32 [32, 8, 36], P('bulk')
- coupling: float32 [20, 32, 6, 128], P(None, 'bulk'), may hold values from -15 to 15
- diag_blocks: bfloat16 [20, 32, 128, 128], P(None, 'bulk'), as said below
- diag_normal: float32 [20, 32, 6], P(None, 'bulk'), may hold values from -4 to 4
- off_blocks: bfloat16 [32, 32, 128, 128], P(None, 'bulk'), may hold values from -0.5 to 0.5
- off_row: int32 [32, 32], P(None, 'bulk'), may hold values from 0 to 19, as said below
- off_col: int32 [32, 32], P(None, 'bulk'), may hold values from 0 to 19, as said below
- off_normal: float32 [32, 32, 6], P(None, 'bulk'), may hold values from -4 to 4
- off_count: int32 [32], P('bulk'), may hold values from 4 to 32, as said below
- fluct_state: bfloat16 [65536, 3072], P(('sec', 'bulk')), as said below
Outputs:
- residual: float32 [3, 16384], P(None, ('sec', 'bulk'))
- product: float32 [3, 16384], P(None, ('sec', 'bulk'))
- update: float32 [3, 16384], P(None, ('sec', 'bulk'))
- fluct_new: bfloat16 [65536, 3072], P(('sec', 'bulk'))
Inputs may be any that keep to these rules, and one draw needn't show every extreme that they name: o = point_map[e] // 512 is the serving device, in the order of sec and bulk with sec slowest, and p = point_map[e] % 512 its slot; values are distinct. Device s sends exactly 4 points to every server, 1 of them in volumes with c block rows for each c = 1 .. 4: among the server's slots whose volume has c block rows, taken in increasing order, the one numbered s. `vol_blocks`: each group has 2 volumes of each size from 1 to 4, so 20 block rows in all. `off_row`: A contact's row and column lie in the block rows of one volume of its group, and differ unless that volume has one block row. `off_col`: see off_row. Slots below off_count of a group are in use, the others are not; a multiple of 4, and one group uses all slots. `diag_blocks`: the diagonal entries of every diagonal block lie between 2.5 and 6.5. `fluct_state`: levels a >= the block rows of the point's volume are zero.
All inputs are finite; a program needn't handle non-finite values.
Results may differ from a plain program's by a relative error of at most 0.001.
The roundings to bfloat16 on the way count: a program that leaves them out, or rounds other values in their place, can miss the bound.
Values may be sent and summed in bfloat16 or wider, within the bound.
A program may use at most 128 MiB of HBM per device.

v0:
```python
import jax
import jax.numpy as jnp
from jax import lax
from jax.sharding import PartitionSpec as P

BS = 128
NBMAX = 4
VOL_GRP = 8
GPV_DEV = 64
SWEEPS = 3
ROWS_GRP = 20


HIGHEST_PREC = lax.Precision.HIGHEST
GAIN_NORMAL = 0.4
CLIP_RMS = 1.0


def strain_of(shape_grads, nodal):
    shaped = shape_grads.reshape(4, 3, -1)
    grad_x, grad_y, grad_z = (shaped[:, 0], shaped[:, 1], shaped[:, 2])
    disp_x, disp_y, disp_z = (nodal[0], nodal[1], nodal[2])
    return jnp.stack(
        [
            jnp.sum(grad_x * disp_x, axis=0),
            jnp.sum(grad_y * disp_y, axis=0),
            jnp.sum(grad_z * disp_z, axis=0),
            jnp.sum(grad_z * disp_y + grad_y * disp_z, axis=0),
            jnp.sum(grad_z * disp_x + grad_x * disp_z, axis=0),
            jnp.sum(grad_y * disp_x + grad_x * disp_y, axis=0),
        ]
    )


def forces_of(shape_grads, stress):
    shaped = shape_grads.reshape(4, 3, -1)
    grad_x, grad_y, grad_z = (shaped[:, 0], shaped[:, 1], shaped[:, 2])
    force_x = grad_x * stress[0] + grad_z * stress[4] + grad_y * stress[5]
    force_y = grad_y * stress[1] + grad_z * stress[3] + grad_x * stress[5]
    force_z = grad_z * stress[2] + grad_y * stress[3] + grad_x * stress[4]
    return jnp.stack([force_x, force_y, force_z])


def apply_tangent(tangent_cols, strain):
    return jnp.sum(tangent_cols.reshape(6, 6, -1) * strain[None, :, :], axis=1)


def assemble(forces, node_ids, node_total):
    flat_ids = node_ids.reshape(-1)
    return jnp.stack(
        [
            jax.ops.segment_sum(forces[component].reshape(-1), flat_ids, num_segments=node_total)
            for component in range(3)
        ]
    )


def row_layout(vol_sizes):
    row_ends = jnp.cumsum(vol_sizes)
    starts = row_ends - vol_sizes
    row_ids = jnp.arange(ROWS_GRP, dtype=jnp.int32)
    row_volume = jnp.sum((row_ids[:, None] >= row_ends[None, :]).astype(jnp.int32), axis=1)
    onehot = jnp.arange(VOL_GRP, dtype=jnp.int32)[:, None] == row_volume[None, :]
    row_level = row_ids - jnp.sum(jnp.where(onehot, starts[:, None], 0), axis=0)
    return (row_volume, onehot.astype(jnp.float32), row_volume * NBMAX + row_level, row_level)


def state_rows(state_slots, gather_index):
    shaped = state_slots.reshape(VOL_GRP, GPV_DEV, NBMAX, BS, 6)
    reordered = jnp.transpose(shaped, (0, 2, 3, 1, 4)).reshape(VOL_GRP * NBMAX, BS, GPV_DEV * 6)
    return reordered[gather_index]


def rows_state(row_values, gather_index):
    padded = (
        jnp.zeros((VOL_GRP * NBMAX, BS, GPV_DEV * 6), row_values.dtype)
        .at[gather_index]
        .set(row_values)
    )
    shaped = padded.reshape(VOL_GRP, NBMAX, BS, GPV_DEV, 6)
    return jnp.transpose(shaped, (0, 3, 1, 2, 4)).reshape(VOL_GRP * GPV_DEV, NBMAX * BS * 6)


def slot_layout(vol_sizes, per_class):
    vol_ids = jnp.arange(VOL_GRP, dtype=jnp.int32)
    earlier = (vol_sizes[None, :] == vol_sizes[:, None]) & (vol_ids[None, :] < vol_ids[:, None])
    vol_rank = jnp.sum(earlier.astype(jnp.int32), axis=1)
    column_ids = jnp.arange(GPV_DEV, dtype=jnp.int32)
    slot_rank = (vol_rank[:, None] * GPV_DEV + column_ids[None, :]).reshape(-1)
    slot_sizes = jnp.broadcast_to(vol_sizes[:, None], (VOL_GRP, GPV_DEV)).reshape(-1)
    slot_ids = jnp.arange(VOL_GRP * GPV_DEV, dtype=jnp.int32)
    slot_source = slot_rank // per_class
    recv_order = jnp.argsort(slot_source * (VOL_GRP * GPV_DEV) + slot_ids)
    recv_position = jnp.zeros_like(slot_ids).at[recv_order].set(slot_ids)
    return (slot_sizes, slot_source, recv_order, recv_position)


def contact_terms(applied, fluct_low, off_blk, off_rows, off_cols, off_scale_cols):
    contrib = jnp.einsum(
        "oab,obc->oac", off_blk, fluct_low[off_cols], preferred_element_type=jnp.float32
    )
    result = applied.at[off_rows].add(contrib * off_scale_cols[:, None, :])
    return result


def micro_solve(
    strain_slots,
    fluctuation,
    vol_sizes,
    layout,
    c_affine,
    coupling,
    diag_blk,
    diag_nrm,
    off_blk,
    off_rows,
    off_cols,
    off_nrm,
    live_count,
):
    slot_total = off_blk.shape[0]
    row_volume, onehot, gather_index, row_level = layout
    strain_vg = strain_slots.astype(jnp.float32).reshape(VOL_GRP, GPV_DEV, 6)
    strain_rows = jnp.einsum("vr,vgk->rgk", onehot, strain_vg, precision=HIGHEST_PREC)
    diag_scale = 1.0 + GAIN_NORMAL * jnp.tanh(
        jnp.einsum("rk,rgk->rg", diag_nrm, strain_rows, precision=HIGHEST_PREC)
    )
    diag_cols = jnp.repeat(diag_scale, 6, axis=1)
    off_strain = strain_vg[row_volume[off_rows]]
    live_mask = (jnp.arange(slot_total, dtype=jnp.int32) < live_count).astype(jnp.float32)
    off_scale = (
        1.0
        + GAIN_NORMAL
        * jnp.tanh(jnp.einsum("ok,ogk->og", off_nrm, off_strain, precision=HIGHEST_PREC))
    ) * live_mask[:, None]
    off_scale_cols = jnp.repeat(off_scale, 6, axis=1)
    diag_vals = jnp.diagonal(diag_blk, axis1=1, axis2=2).astype(jnp.float32)
    load_rows = jnp.tile(jnp.swapaxes(coupling, 1, 2), (1, 1, GPV_DEV))
    denominator = diag_vals[:, :, None] * diag_cols[:, None, :]
    for sweep_index in range(SWEEPS):
        fluct_low = fluctuation.astype(jnp.bfloat16)
        applied = (
            jnp.einsum("rab,rbc->rac", diag_blk, fluct_low, preferred_element_type=jnp.float32)
            * diag_cols[:, None, :]
        )
        applied = contact_terms(applied, fluct_low, off_blk, off_rows, off_cols, off_scale_cols)
        fluctuation = fluctuation + (load_rows - applied) / denominator
    projection = jnp.einsum("rid,rdc->ric", coupling, fluctuation, precision=HIGHEST_PREC)
    vol_proj = jnp.einsum("vr,ric->vic", onehot, projection, precision=HIGHEST_PREC)
    vol_proj = vol_proj / (vol_sizes.astype(jnp.float32) * BS)[:, None, None]
    tangent = c_affine.reshape(VOL_GRP, 6, 1, 6) - vol_proj.reshape(VOL_GRP, 6, GPV_DEV, 6)
    tangent = (
        jnp.transpose(tangent, (0, 2, 1, 3)).reshape(VOL_GRP * GPV_DEV, 36).astype(jnp.bfloat16)
    )
    return (tangent, fluctuation.astype(jnp.bfloat16))


def on_device(
    displacement,
    nodal_load,
    connectivity,
    shape_grads,
    elem_volume,
    point_map,
    vol_blocks,
    c_affine,
    coupling,
    diag_blocks,
    diag_normal,
    off_blocks,
    off_row,
    off_col,
    off_normal,
    off_count,
    fluct_state,
):
    elem_count = connectivity.shape[1]
    node_count = displacement.shape[1]
    state_width = fluct_state.shape[1]
    devices = lax.axis_size(("sec", "bulk"))
    per_peer = elem_count // devices
    element_ids = jnp.arange(elem_count, dtype=jnp.int32)
    strain = strain_of(shape_grads, displacement[:, connectivity])
    send_order = jnp.argsort(point_map)
    send_position = jnp.zeros_like(element_ids).at[send_order].set(element_ids)
    own_sizes = vol_blocks[0]
    layout = row_layout(own_sizes)
    slot_sizes, slot_source, recv_order, recv_position = slot_layout(own_sizes, per_peer // NBMAX)
    strain_send = strain.T[send_order].astype(jnp.bfloat16).reshape(devices, per_peer * 6)
    state_send = fluct_state[send_order].reshape(devices, per_peer * state_width)
    strain_got, state_got = (
        lax.all_to_all(strain_send, ("sec", "bulk"), split_axis=0, concat_axis=0, tiled=True),
        lax.all_to_all(state_send, ("sec", "bulk"), split_axis=0, concat_axis=0, tiled=True),
    )
    strain_slots = strain_got.reshape(elem_count, 6)[recv_position]
    state_slots = state_got.reshape(elem_count, state_width)[recv_position]
    fluctuation = state_rows(state_slots, layout[2]).astype(jnp.float32)
    tangent, fluct_rows = micro_solve(
        strain_slots,
        fluctuation,
        own_sizes,
        layout,
        c_affine[0],
        coupling[:, 0],
        diag_blocks[:, 0],
        diag_normal[:, 0],
        off_blocks[:, 0],
        off_row[:, 0],
        off_col[:, 0],
        off_normal[:, 0],
        off_count[0],
    )
    tangent_send = tangent[recv_order].reshape(devices, per_peer * 36)
    state_back = rows_state(fluct_rows, layout[2])[recv_order].reshape(
        devices, per_peer * state_width
    )
    tangent_got, state_home = (
        lax.all_to_all(tangent_send, ("sec", "bulk"), split_axis=0, concat_axis=0, tiled=True),
        lax.all_to_all(state_back, ("sec", "bulk"), split_axis=0, concat_axis=0, tiled=True),
    )
    tangent_elem = tangent_got.reshape(elem_count, 36)[send_position]
    fluct_new = state_home.reshape(elem_count, state_width)[send_position]
    tangent_cols = tangent_elem.astype(jnp.float32).T
    weights = elem_volume[None, :]
    stress = apply_tangent(tangent_cols, strain)
    residual = (
        assemble(forces_of(shape_grads, weights * stress), connectivity, node_count) - nodal_load
    )
    norm_sq = lax.psum(jnp.sum(residual * residual), ("sec", "bulk"))
    root_mean = jnp.sqrt(norm_sq / (3.0 * node_count * devices) + 1e-06)
    update = -jnp.minimum(1.0, CLIP_RMS / root_mean) * residual
    trial_strain = strain_of(shape_grads, residual[:, connectivity])
    product = assemble(
        forces_of(shape_grads, weights * apply_tangent(tangent_cols, trial_strain)),
        connectivity,
        node_count,
    )
    return (residual, product, update, fluct_new)


def solution(mesh):
    return jax.shard_map(
        on_device,
        mesh=mesh,
        in_specs=(
            P(None, ("sec", "bulk")),
            P(None, ("sec", "bulk")),
            P(None, ("sec", "bulk")),
            P(None, ("sec", "bulk")),
            P(("sec", "bulk")),
            P(("sec", "bulk")),
            P("bulk", None),
            P("bulk", None, None),
            P(None, "bulk", None, None),
            P(None, "bulk", None, None),
            P(None, "bulk", None),
            P(None, "bulk", None, None),
            P(None, "bulk"),
            P(None, "bulk"),
            P(None, "bulk", None),
            P("bulk"),
            P(("sec", "bulk"), None),
        ),
        out_specs=(
            P(None, ("sec", "bulk")),
            P(None, ("sec", "bulk")),
            P(None, ("sec", "bulk")),
            P(("sec", "bulk"), None),
        ),
        check_vma=False,
    )
```

profile of v0, /device:TPU:1, one launch (start us, length us, event | category | flops | bytes accessed | tf_op | source)
XLA Modules:
  0.0 653.3 jit_solution(12383099362356795251)
XLA Ops:
  3.1 7.6 %gather_fusion.3 = f32[2048,3]{1,0:T(8,128)} fusion(f32[3,128]{0,1:T(8,128)S(1)} %copy.271, s32[2048]{0:T(1024)S(1)} %broadcast_clamp_fusion), kind=kCustom, calls=%fused_computation.3 | custom fusion | bytes 57344 | tf_op jit(solution)/shard_map/gather | solution.py:183
  12.6 4.4 sort.31
  19.2 11.5 %all-to-all-start.1 = ((bf16[128,1,24]{2,1,0:T(2,128)(2,1)}), bf16[128,1,24]{2,1,0:T(2,128)(2,1)S(1)}, u32[]{:S(2)}, u32[]{:S(2)}) async-start(bf16[128,1,24]{2,1,0:T(2,128)(2,1)} %convert_element_type.86), calls=%async_computation.1 | async-start | bytes 131072 | tf_op jit(solution)/shard_map/all_to_all | solution.py:192
  31.8 3.8 sort.32
  36.2 4.7 copy.268
  43.1 3.8 gather_fusion
  46.9 16.5 %all_to_all.29 = bf16[128,1,12288]{2,1,0:T(2,128)(2,1)} reshape(bf16[512,3072]{1,0:T(8,128)(2,1)} %gather_fusion) | data formatting | bytes 6291456 | tf_op jit(solution)/shard_map/all_to_all | solution.py:193
  64.0 19.0 %reduce.8 = bf16[128,12288]{1,0:T(8,128)(2,1)S(1)} reduce(bf16[128,1,12288]{2,1,0:T(2,128)(2,1)} %all_to_all.29, bf16[]{:T(256)} %broadcast.250), dimensions={1}, to_apply=%all_to_all.29.reduce_sub_computation | reduce | bytes 6291458 | tf_op jit(solution)/shard_map/all_to_all | solution.py:193
  83.0 3.5 reshape.521
  86.5 9.8 %all-to-all-start = ((bf16[128,2,6144]{2,1,0:T(2,128)(2,1)}), bf16[128,2,6144]{2,1,0:T(2,128)(2,1)S(1)}, u32[]{:S(2)}, u32[]{:S(2)}) async-start(bf16[128,2,6144]{2,1,0:T(2,128)(2,1)} %reshape.521), calls=%async_computation | async-start | bytes 6291456 | tf_op jit(solution)/shard_map/all_to_all | solution.py:193
  100.1 5.8 copy.282
  125.0 12.5 %all-to-all-done = bf16[128,2,6144]{2,1,0:T(2,128)(2,1)S(1)} async-done(((bf16[128,2,6144]{2,1,0:T(2,128)(2,1)}), bf16[128,2,6144]{2,1,0:T(2,128)(2,1)S(1)}, u32[]{:S(2)}, u32[]{:S(2)}) %all-to-all-start) | async-done | bytes 3145760 | tf_op jit(solution)/shard_map/all_to_all | solution.py:193
  137.5 7.6 %reshape.522 = bf16[128,1,12288]{2,1,0:T(2,128)(2,1)} reshape(bf16[128,2,6144]{2,1,0:T(2,128)(2,1)S(1)} %all-to-all-done) | data formatting | bytes 6291456
  145.1 20.0 %reduce.2 = bf16[128,12288]{1,0:T(8,128)(2,1)} reduce(bf16[128,1,12288]{2,1,0:T(2,128)(2,1)} %reshape.522, bf16[]{:T(256)} %constant.83), dimensions={1}, to_apply=%all_to_all.23.reduce_sub_computation | reduce | bytes 6291458 | tf_op jit(solution)/shard_map/all_to_all | solution.py:193
  165.1 4.9 reshape.230
  170.0 3.8 gather_fusion.1
  173.8 3.2 copy.264
  177.0 5.6 reshape.231
  182.7 8.4 %copy.265 = bf16[8,4,128,64,6]{2,1,0,4,3:T(4,128)(2,1)S(1)} copy(bf16[8,4,128,64,6]{3,0,4,2,1:T(8,128)(2,1)} %bitcast.303) | data formatting | bytes 6291456 | tf_op jit(solution)/shard_map/transpose | solution.py:70
  191.1 3.4 copy.266
  194.5 3.0 gather_fusion.2
  200.4 5.7 multiply_bitcast_fusion.2
  206.2 6.7 %copy.281 = f32[32,128,384]{2,1,0:T(8,128)} copy(f32[32,128,384]{1,2,0:T(8,128)} %multiply_bitcast_fusion.2) | data formatting | bytes 12582912 | tf_op jit(solution)/shard_map/mul | solution.py:102
  212.8 3.6 multiply_bitcast_fusion.5
  216.4 5.6 copy.280
  222.0 16.1 %scatter_fusion = f32[20,128,384]{2,1,0:T(8,128)} fusion(f32[20,128,384]{2,1,0:T(8,128)} %copy.280, s32[32]{0:T(128)S(1)} %copy-done.20, f32[32,128,384]{2,1,0:T(8,128)} %copy.281), kind=kCustom, calls=%fused_computation.18 | custom fusion | flops 1572864 | bytes 18874496 | tf_op jit(solution)/shard_map/scatter-add | solution.py:102
  238.1 4.9 fusion.53
  243.0 4.3 gather_fusion.10
  247.3 5.2 multiply_bitcast_fusion.4
  252.5 4.6 multiply_bitcast_fusion.1
  257.1 6.6 %copy.289 = f32[32,128,384]{2,1,0:T(8,128)} copy(f32[32,128,384]{1,2,0:T(8,128)} %multiply_bitcast_fusion.1) | data formatting | bytes 12582912 | tf_op jit(solution)/shard_map/mul | solution.py:102
  263.7 5.6 copy.288
  269.2 15.8 %scatter_fusion.1 = f32[20,128,384]{2,1,0:T(8,128)} fusion(f32[20,128,384]{2,1,0:T(8,128)} %copy.288, s32[32]{0:T(128)S(1)} %copy-done.20, f32[32,128,384]{2,1,0:T(8,128)} %copy.289), kind=kCustom, calls=%fused_computation.19 | custom fusion | flops 1572864 | bytes 18874496 | tf_op jit(solution)/shard_map/scatter-add | solution.py:102
  285.1 6.8 %fusion.56 = (bf16[20,128,384]{2,1,0:T(8,128)(2,1)}, f32[20,128,384]{2,1,0:T(8,128)}) fusion(f32[20,128,384]{2,1,0:T(8,128)} %copy.282, f32[20,128,384]{2,1,0:T(8,128)} %scatter_fusion.1, f32[20,384]{1,0:T(8,128)S(1)} %copy.277, f32[20,128]{1,0:T(8,128)S(1)} %copy.283, f32[20,128,384]{2,1,0:T(8,128)} %scatter_fusion, bf16[20,128,384]{2,1,0:T(8,128)(2,1)S(1)} %gather_fusion.2), kind=kLoop, calls=%fused_computation.180 | loop fusion | flops 8847360 | bytes 19701760 | tf_op jit(solution)/shard_map/convert_element_type | solution.py:141
  291.8 4.5 gather_fusion.11
  296.3 3.6 multiply_bitcast_fusion.3
  299.9 4.6 multiply_bitcast_fusion
  304.4 6.6 %copy.295 = f32[32,128,384]{2,1,0:T(8,128)} copy(f32[32,128,384]{1,2,0:T(8,128)} %multiply_bitcast_fusion) | data formatting | bytes 12582912 | tf_op jit(solution)/shard_map/mul | solution.py:102
  311.0 5.6 copy.294
  316.6 15.8 %scatter_fusion.2 = f32[20,128,384]{2,1,0:T(8,128)} fusion(f32[20,128,384]{2,1,0:T(8,128)} %copy.294, s32[32]{0:T(128)S(1)} %copy-done.20, f32[32,128,384]{2,1,0:T(8,128)} %copy.295), kind=kCustom, calls=%fused_computation.20 | custom fusion | flops 1572864 | bytes 18874496 | tf_op jit(solution)/shard_map/scatter-add | solution.py:102
  332.4 6.3 fusion.54
  346.1 6.5 all-to-all-start.2
  354.5 4.5 scatter_fusion.3
  359.0 3.4 copy.306
  362.4 8.9 %copy.307 = bf16[8,64,4,128,6]{1,0,4,3,2:T(8,128)(2,1)} copy(bf16[8,64,4,128,6]{3,2,0,4,1:T(4,128)(2,1)} %bitcast.306) | data formatting | bytes 6291456 | tf_op jit(solution)/shard_map/transpose | solution.py:81
  371.2 9.3 %reshape.240 = bf16[512,3072]{0,1:T(8,128)(2,1)} reshape(bf16[8,64,4,128,6]{1,0,4,3,2:T(8,128)(2,1)} %copy.307) | data formatting | bytes 6291456 | tf_op jit(solution)/shard_map/reshape | solution.py:81
  380.5 3.2 copy.308
  383.7 3.8 gather_fusion.15
  387.5 16.5 %all_to_all.31 = bf16[128,1,12288]{2,1,0:T(2,128)(2,1)} reshape(bf16[512,3072]{1,0:T(8,128)(2,1)} %gather_fusion.15) | data formatting | bytes 6291456 | tf_op jit(solution)/shard_map/all_to_all | solution.py:219
  404.1 19.0 %reduce.9 = bf16[128,12288]{1,0:T(8,128)(2,1)S(1)} reduce(bf16[128,1,12288]{2,1,0:T(2,128)(2,1)} %all_to_all.31, bf16[]{:T(256)} %broadcast.250), dimensions={1}, to_apply=%all_to_all.31.reduce_sub_computation | reduce | bytes 6291458 | tf_op jit(solution)/shard_map/all_to_all | solution.py:219
  423.1 3.5 reshape.523
  426.6 9.9 %all-to-all-start.3 = ((bf16[128,2,6144]{2,1,0:T(2,128)(2,1)}), bf16[128,2,6144]{2,1,0:T(2,128)(2,1)S(1)}, u32[]{:S(2)}, u32[]{:S(2)}) async-start(bf16[128,2,6144]{2,1,0:T(2,128)(2,1)} %reshape.523), calls=%async_computation.3 | async-start | bytes 6291456 | tf_op jit(solution)/shard_map/all_to_all | solution.py:219
  440.9 14.8 %scatter_custom_fusion.5 = f32[128]{0:T(128)S(1)} fusion(s32[2048]{0:T(1024)} %bitcast.361, f32[2048]{0:T(1024)S(1)} %get-tuple-element.53, f32[]{:T(128)} %constant.15.clone.1), kind=kCustom, calls=%fused_computation.175 | custom fusion | flops 2048 | bytes 1024 | tf_op jit(solution)/shard_map/scatter-add | solution.py:52
  455.7 15.2 %scatter_custom_fusion.6 = f32[128]{0:T(128)S(1)} fusion(s32[2048]{0:T(1024)} %bitcast.362, f32[2048]{0:T(1024)S(1)} %get-tuple-element.55, f32[]{:T(128)} %constant.15.clone.1), kind=kCustom, calls=%fused_computation.173 | custom fusion | flops 2048 | bytes 1024 | tf_op jit(solution)/shard_map/scatter-add | solution.py:52
  470.9 14.8 %scatter_custom_fusion.7 = f32[128]{0:T(128)S(1)} fusion(s32[2048]{0:T(1024)} %bitcast.363, f32[2048]{0:T(1024)S(1)} %get-tuple-element.54, f32[]{:T(128)} %constant.15.clone.1), kind=kCustom, calls=%fused_computation.171 | custom fusion | flops 2048 | bytes 1024 | tf_op jit(solution)/shard_map/scatter-add | solution.py:52
  487.3 67.1 %psum.7 = f32[]{:T(128)} all-reduce(f32[]{:T(128)} %get-tuple-element.46), channel_id=1, replica_groups=mesh['sec'=4,'bulk'=32] {'sec','bulk'}, use_global_device_ids=true, to_apply=%region_32.33 | all-reduce | flops 1 | bytes 8 | tf_op jit(solution)/shard_map/psum | solution.py:229
  554.4 8.3 %gather_fusion.14 = f32[2048,3]{1,0:T(8,128)} fusion(f32[3,128]{0,1:T(8,128)S(1)} %get-tuple-element.47, s32[2048]{0:T(1024)} %copy-done.13), kind=kCustom, calls=%fused_computation.14 | custom fusion | bytes 57344 | tf_op jit(solution)/shard_map/gather | solution.py:232
  568.7 14.8 %scatter_custom_fusion.8 = f32[128]{0:T(128)S(1)} fusion(s32[2048]{0:T(1024)} %bitcast.364, f32[2048]{0:T(1024)S(1)} %get-tuple-element.50, f32[]{:T(128)} %constant.15.clone.1), kind=kCustom, calls=%fused_computation.169 | custom fusion | flops 2048 | bytes 1024 | tf_op jit(solution)/shard_map/scatter-add | solution.py:52
  583.5 14.8 %scatter_custom_fusion.9 = f32[128]{0:T(128)S(1)} fusion(s32[2048]{0:T(1024)} %bitcast.365, f32[2048]{0:T(1024)S(1)} %get-tuple-element.52, f32[]{:T(128)} %constant.15.clone.1), kind=kCustom, calls=%fused_computation.167 | custom fusion | flops 2048 | bytes 1024 | tf_op jit(solution)/shard_map/scatter-add | solution.py:52
  598.3 15.0 %scatter_custom_fusion.10 = f32[128]{0:T(128)S(1)} fusion(s32[2048]{0:T(1024)} %bitcast.366, f32[2048]{0:T(1024)S(1)} %get-tuple-element.51, f32[]{:T(128)} %constant.15.clone.1), kind=kCustom, calls=%fused_computation.165 | custom fusion | flops 2048 | bytes 1024 | tf_op jit(solution)/shard_map/scatter-add | solution.py:52
  613.9 7.6 %reshape.524 = bf16[128,1,12288]{2,1,0:T(2,128)(2,1)} reshape(bf16[128,2,6144]{2,1,0:T(2,128)(2,1)S(1)} %all-to-all-done.3) | data formatting | bytes 6291456
  621.5 18.3 %reduce.5 = bf16[128,12288]{1,0:T(8,128)(2,1)S(1)} reduce(bf16[128,1,12288]{2,1,0:T(2,128)(2,1)} %reshape.524, bf16[]{:T(256)} %constant.83), dimensions={1}, to_apply=%all_to_all.28.reduce_sub_computation | reduce | bytes 6291458 | tf_op jit(solution)/shard_map/all_to_all | solution.py:219
  639.9 3.8 reshape.241
  643.7 9.5 %gather_fusion.16 = bf16[512,3072]{1,0:T(8,128)(2,1)} fusion(bf16[512,3072]{1,0:T(8,128)(2,1)} %reshape.241, s32[1024]{0:T(1024)S(1)} %copy-done.16), kind=kCustom, calls=%fused_computation.16 | custom fusion | bytes 6293504 | tf_op jit(solution)/shard_map/gather | solution.py:222
  (200 shorter events, 56.6 us)
Async XLA Ops:
  0.6 42.5 %copy-start = (bf16[512,3072]{1,0:T(8,128)(2,1)S(1)}, bf16[512,3072]{1,0:T(8,128)(2,1)}, u32[]{:S(2)}) copy-start(bf16[512,3072]{1,0:T(8,128)(2,1)} %param.33) | copy-start | bytes 9437188
  1.6 10.8 %copy-start.10 = (f32[4,1,512]{2,1,0:T(1,128)}, f32[4,1,512]{2,1,0:T(1,128)S(1)}, u32[]{:S(2)}) copy-start(f32[4,1,512]{2,1,0:T(1,128)S(1)} %get-tuple-element.58) | copy-start | bytes 24580
  2.3 10.1 %copy-start.13 = (s32[2048]{0:T(1024)}, s32[2048]{0:T(1024)S(1)}, u32[]{:S(2)}) copy-start(s32[2048]{0:T(1024)S(1)} %broadcast_clamp_fusion) | copy-start | bytes 24580
  10.8 32.1 %copy-start.29 = (s32[1,8]{1,0:T(1,128)S(1)}, s32[1,8]{1,0:T(1,128)}, u32[]{:S(2)}) copy-start(s32[1,8]{1,0:T(1,128)} %param.23) | copy-start | bytes 100
  12.4 4.7 copy-start.11
  19.2 67.3 %all-to-all-start.1 = ((bf16[128,1,24]{2,1,0:T(2,128)(2,1)}), bf16[128,1,24]{2,1,0:T(2,128)(2,1)S(1)}, u32[]{:S(2)}, u32[]{:S(2)}) async-start(bf16[128,1,24]{2,1,0:T(2,128)(2,1)} %convert_element_type.86), calls=%async_computation.1 | async-start | bytes 131072 | tf_op jit(solution)/shard_map/all_to_all | solution.py:192
  36.2 60.1 %copy-start.19 = (s32[32]{0:T(128)}, s32[32]{0:T(128)S(1)}, u32[]{:S(2)}) copy-start(s32[32]{0:T(128)S(1)} %fusion.37) | copy-start | bytes 388
  86.5 9.8 %copy-start.23 = (f32[32,1,6]{0,1,2:T(1,128)S(1)}, f32[32,1,6]{0,1,2:T(1,128)}, u32[]{:S(2)}) copy-start(f32[32,1,6]{0,1,2:T(1,128)} %param.31) | copy-start | bytes 2308
  86.5 10.6 %copy-start.24 = (f32[20,1,6]{0,1,2:T(1,128)S(1)}, f32[20,1,6]{0,1,2:T(1,128)}, u32[]{:S(2)}) copy-start(f32[20,1,6]{0,1,2:T(1,128)} %param.27) | copy-start | bytes 1444
  86.5 11.2 %copy-start.9 = (f32[20,1,6,128]{3,1,2,0:T(1,128)S(1)}, f32[20,1,6,128]{3,1,2,0:T(1,128)}, u32[]{:S(2)}) copy-start(f32[20,1,6,128]{3,1,2,0:T(1,128)} %param.25) | copy-start | bytes 184324
  86.5 50.9 %all-to-all-start = ((bf16[128,2,6144]{2,1,0:T(2,128)(2,1)}), bf16[128,2,6144]{2,1,0:T(2,128)(2,1)S(1)}, u32[]{:S(2)}, u32[]{:S(2)}) async-start(bf16[128,2,6144]{2,1,0:T(2,128)(2,1)} %reshape.521), calls=%async_computation | async-start | bytes 6291456 | tf_op jit(solution)/shard_map/all_to_all | solution.py:193
  100.1 8.3 %copy-start.22 = (f32[1,8,36]{2,1,0:T(8,128)S(1)}, f32[1,8,36]{2,1,0:T(8,128)}, u32[]{:S(2)}) copy-start(f32[1,8,36]{2,1,0:T(8,128)} %param.24) | copy-start | bytes 3460
  100.1 13.4 %copy-start.28 = (s32[32,1]{0,1:T(1,128)S(1)}, s32[32,1]{0,1:T(1,128)}, u32[]{:S(2)}) copy-start(s32[32,1]{0,1:T(1,128)} %param.30) | copy-start | bytes 388
  112.8 7.6 %copy-start.17 = (s32[1024]{0:T(1024)}, s32[1024]{0:T(1024)S(1)}, u32[]{:S(2)}) copy-start(s32[1024]{0:T(1024)S(1)} %pad_clamp_fusion.6) | copy-start | bytes 12292
  112.9 2.5 copy-start.25
  165.1 4.9 copy-start.18
  197.5 2.9 copy-start.6
  206.2 6.7 %copy-start.5 = (bf16[20,1,128,128]{3,2,1,0:T(8,128)(2,1)S(1)}, bf16[20,1,128,128]{3,2,1,0:T(8,128)(2,1)}, u32[]{:S(2)}) copy-start(bf16[20,1,128,128]{3,2,1,0:T(8,128)(2,1)} %param.26) | copy-start | bytes 1966084
  216.4 5.6 copy-start.20
  247.3 5.2 copy-start.4
  247.3 5.2 copy-start.7
  291.8 4.5 copy-start.2
  296.3 3.6 copy-start.3
  296.3 3.6 copy-start.8
  338.7 2.6 copy-start.30
  338.7 4.4 copy-start.12
  341.3 11.4 %copy-start.21 = (s32[512]{0:T(512)S(1)}, s32[512]{0:T(512)}, u32[]{:S(2)}) copy-start(s32[512]{0:T(512)} %compare_select_fusion.1) | copy-start | bytes 6148
  341.3 11.4 %copy-start.14 = (s32[4,512]{1,0:T(4,128)S(1)}, s32[4,512]{1,0:T(4,128)}, u32[]{:S(2)}) copy-start(s32[4,512]{1,0:T(4,128)} %param.19) | copy-start | bytes 24580
  341.3 12.0 %copy-start.27 = (f32[3,128]{1,0:T(4,128)S(1)}, f32[3,128]{1,0:T(4,128)}, u32[]{:S(2)}) copy-start(f32[3,128]{1,0:T(4,128)} %param.18) | copy-start | bytes 4612
  343.1 11.4 %copy-start.26 = (s32[20]{0:T(128)S(1)}, s32[20]{0:T(128)}, u32[]{:S(2)}) copy-start(s32[20]{0:T(128)} %copy-done.25) | copy-start | bytes 244
  346.1 80.5 %all-to-all-start.2 = ((bf16[128,1,144]{2,1,0:T(2,128)(2,1)}), bf16[128,1,144]{2,1,0:T(2,128)(2,1)S(1)}, u32[]{:S(2)}, u32[]{:S(2)}) async-start(bf16[128,1,144]{2,1,0:T(2,128)(2,1)} %all_to_all.30), calls=%async_computation.2 | async-start | bytes 262144 | tf_op jit(solution)/shard_map/all_to_all | solution.py:218
  352.7 84.4 %copy-start.15 = (s32[1024]{0:T(1024)}, s32[1024]{0:T(1024)S(1)}, u32[]{:S(2)}) copy-start(s32[1024]{0:T(1024)S(1)} %pad_clamp_fusion) | copy-start | bytes 12292
  426.6 187.3 %all-to-all-start.3 = ((bf16[128,2,6144]{2,1,0:T(2,128)(2,1)}), bf16[128,2,6144]{2,1,0:T(2,128)(2,1)S(1)}, u32[]{:S(2)}, u32[]{:S(2)}) async-start(bf16[128,2,6144]{2,1,0:T(2,128)(2,1)} %reshape.523), calls=%async_computation.3 | async-start | bytes 6291456 | tf_op jit(solution)/shard_map/all_to_all | solution.py:219
  639.9 3.8 copy-start.16
  643.7 9.5 %copy-start.1 = (bf16[512,3072]{1,0:T(8,128)(2,1)S(1)}, bf16[512,3072]{1,0:T(8,128)(2,1)}, u32[]{:S(2)}) copy-start(bf16[512,3072]{1,0:T(8,128)(2,1)} %param.33) | copy-start | bytes 9437188
where the time goes:
time: 665 us; the launch traced here: 653 us
  other arithmetic  253 us (38%)
  local copies, waits for them, and re-layouts  249 us (37%)
  blocking collectives  67.1 us (10%)
  starting transfers between devices  37.6 us (6%)
  matrix products  30.9 us (5%)
  waiting for transfers between devices  12.5 us (2%)
    scatter-add x6, other arithmetic, assemble(): jax.ops.segment_sum(forces[component].reshape(-1), flat_ids, num_segments...  89.4 us
    psum x1, blocking collectives, on_device(): norm_sq = lax.psum(jnp.sum(residual * residual), ('sec', 'bulk'))  67.1 us
    scatter-add x3, other arithmetic, contact_terms(): result = applied.at[off_rows].add(contrib * off_scale_cols[:, None, :])  47.7 us
    all_to_all x2, other arithmetic, on_device(): lax.all_to_all(state_send, ('sec', 'bulk'), split_axis=0, concat_axis=0,...  39 us
    all_to_all x2, other arithmetic, on_device(): lax.all_to_all(state_back, ('sec', 'bulk'), split_axis=0, concat_axis=0,...  37.3 us
    unnamed x100, local copies, waits for them, and re-layouts  31.3 us
    mul x5, local copies, waits for them, and re-layouts, contact_terms(): result = applied.at[off_rows].add(contrib * off_scale_cols[:, None, :])  21.6 us
    mul x5, local copies, waits for them, and re-layouts, micro_solve(): jnp.einsum('rab,rbc->rac', diag_blk, fluct_low, preferred_element_type=jn...  18.4 us
  transfers between devices with their start and end apart: 4, of which 1 were waited for; matrix products, arithmetic and copies ran while one was open for 36% of the time, Pallas kernels for 0%

commit v1 on v0

v1 whole, which is shorter than its diff:
```python
import jax
import jax.numpy as jnp
from jax import lax
from jax.experimental import pallas as pl
from jax.experimental.pallas import tpu as pltpu
from jax.sharding import PartitionSpec as P

F32 = jnp.float32
BF16 = jnp.bfloat16
I32 = jnp.int32
N_DEV = 128
ELEM = 512
NODE = 128
LEVEL = 768
MSG = 64
SWEEPS = 3
ROWS = 20
OFF = 32
MESH = pl.DeviceIdType.MESH
BASE = (0, 6, 18, 36)
SLOT0 = (0, 2, 6, 12)
STRIDE_PEER = 37


def dot_nt(a, b):
    return lax.dot_general(a, b, (((1,), (1,)), ((), ())), preferred_element_type=F32)


def dot_nn(a, b):
    return lax.dot_general(a, b, (((1,), (0,)), ((), ())), preferred_element_type=F32)


def iota(shape, dim):
    return lax.broadcasted_iota(I32, shape, dim)


def static_row(c, h, a):
    return SLOT0[c] + h * (c + 1) + a


def my_position():
    sec = lax.axis_index("sec")
    bulk = lax.axis_index("bulk")
    return sec, bulk, sec * 32 + bulk


def peer_of(step, sec, bulk):
    d = lax.rem(step * STRIDE_PEER, N_DEV)
    ty = lax.rem(sec + d // 32, 4)
    tx = lax.rem(bulk // 8 + lax.rem(d // 8, 4), 4)
    tz = lax.rem(lax.rem(bulk // 2, 4) + lax.rem(d // 2, 4), 4)
    tc = lax.rem(lax.rem(bulk, 2) + lax.rem(d, 2), 2)
    tb = (tx * 4 + tz) * 2 + tc
    return ty, tb, ty * 32 + tb


def greet_all(barrier, sec, bulk):
    def greet(step, carry):
        ty, tb, _ = peer_of(step, sec, bulk)
        pl.semaphore_signal(barrier, inc=1, device_id=(ty, tb), device_id_type=MESH)
        return carry

    lax.fori_loop(1, N_DEV, greet, 0)


def split3(nodal, scratch):
    high = nodal.astype(BF16).astype(F32)
    rest = nodal - high
    middle = rest.astype(BF16).astype(F32)
    low = rest - middle
    scratch[...] = jnp.zeros_like(scratch)
    rows = nodal.shape[0]
    scratch[0:rows, :] = high
    scratch[8 : 8 + rows, :] = middle
    scratch[16 : 16 + rows, :] = low
    return scratch[...].astype(BF16)


def node_onehot(conn_ref, a):
    ids = conn_ref[a : a + 1, :]
    return jnp.where(iota((NODE, ELEM), 0) == ids, 1.0, 0.0).astype(BF16)


def gather_nodes(nodal, conn_ref, scratch):
    parts = split3(nodal, scratch)
    out = []
    for a in range(4):
        got = dot_nn(parts, node_onehot(conn_ref, a))
        out.append(got[0:8] + got[8:16] + got[16:24])
    return out


def strain_rows(moved, grads_ref):
    g = [[grads_ref[3 * a + k : 3 * a + k + 1, :] for k in range(3)] for a in range(4)]
    u = [[moved[a][k : k + 1, :] for k in range(3)] for a in range(4)]

    def total(terms):
        out = terms[0]
        for t in terms[1:]:
            out = out + t
        return out

    return [
        total([g[a][0] * u[a][0] for a in range(4)]),
        total([g[a][1] * u[a][1] for a in range(4)]),
        total([g[a][2] * u[a][2] for a in range(4)]),
        total([g[a][2] * u[a][1] + g[a][1] * u[a][2] for a in range(4)]),
        total([g[a][2] * u[a][0] + g[a][0] * u[a][2] for a in range(4)]),
        total([g[a][1] * u[a][0] + g[a][0] * u[a][1] for a in range(4)]),
    ]


def make_spread(spread):
    m = iota((LEVEL, LEVEL), 0)
    n = iota((LEVEL, LEVEL), 1)
    spread[...] = jnp.where(m == lax.rem(n, 128) * 6 + n // 128, 1.0, 0.0).astype(BF16)


def pack_kernel(
    disp, conn, grads, pmap, state_hbm, got,
    state, stage, send, spread, srows, small, load_sem, own_sem, send_sem, recv_sem,
):
    sec, bulk, me = my_position()
    barrier = pltpu.get_barrier_semaphore()
    load = pltpu.make_async_copy(state_hbm, state, load_sem)
    load.start()
    greet_all(barrier, sec, bulk)

    strain = strain_rows(gather_nodes(disp[...], conn, small), grads)
    srows[...] = jnp.zeros_like(srows)
    for i in range(6):
        srows[i : i + 1, :] = strain[i]
    where_to = pmap[...]
    owner = where_to // ELEM
    volume = lax.rem(where_to, ELEM) // 64
    srows[8:9, :] = volume.astype(F32)
    strain_low = srows[...].astype(BF16)
    make_spread(spread)
    load.wait()

    ones = jnp.ones((16, LEVEL), BF16)
    levels = jnp.zeros((1, ELEM), I32)
    for a in range(4):
        weight = dot_nt(ones, jnp.abs(state[:, a * LEVEL : (a + 1) * LEVEL]))[0:1, :]
        levels = jnp.where(weight > 0.0, a + 1, levels)
    key = (owner * 4096 + levels * 512 + iota((1, ELEM), 1)).astype(F32)
    key_col = jnp.transpose(jnp.broadcast_to(key, (128, ELEM)))
    order = []
    for m in range(4):
        part = key[:, m * 128 : (m + 1) * 128]
        order.append(jnp.sum(jnp.where(key_col < part, 1.0, 0.0), axis=0, keepdims=True))
    order = jnp.concatenate(order, axis=1).astype(I32)

    for k in range(4):
        pick = jnp.where(order == iota((N_DEV, ELEM), 0) * 4 + k, 1.0, 0.0).astype(BF16)
        for a in range(k + 1):
            mine = dot_nn(pick, state[:, a * LEVEL : (a + 1) * LEVEL]).astype(BF16)
            flat = dot_nn(mine, spread[...])
            for j in range(6):
                stage[pl.ds(BASE[k] + a * 6 + j, N_DEV, stride=MSG), :] = flat[
                    :, j * 128 : (j + 1) * 128
                ]
        stage[pl.ds(60 + k, N_DEV, stride=MSG), :] = dot_nt(pick, strain_low)

    def lower(i, carry):
        send[pl.ds(i * 2, 2)] = (
            stage[pl.ds(pl.multiple_of(i * 2 * MSG, 2 * MSG), 2 * MSG), :]
            .astype(BF16)
            .reshape(2, MSG, 128)
        )
        return carry

    lax.fori_loop(0, N_DEV // 2, lower, 0)
    own = pltpu.make_async_copy(send.at[me], got.at[me], own_sem)
    own.start()
    pl.semaphore_wait(barrier, N_DEV - 1)

    def push(step, carry):
        ty, tb, t = peer_of(step, sec, bulk)
        pltpu.make_async_remote_copy(
            src_ref=send.at[t],
            dst_ref=got.at[me],
            send_sem=send_sem,
            recv_sem=recv_sem,
            device_id=(ty, tb),
            device_id_type=MESH,
        ).start()
        return carry

    lax.fori_loop(1, N_DEV, push, 0)
    own.wait()
    rest = send.at[pl.ds(0, N_DEV - 1)]
    pltpu.make_async_copy(rest, rest, send_sem).wait()
    landed = got.at[pl.ds(0, N_DEV - 1)]
    pltpu.make_async_copy(landed, landed, recv_sem).wait()


def solve_kernel(
    got, vols, coupling, diag, off, diag_n, off_n, off_row, off_col, off_count, affine,
    back,
    stage, state, low, chain, mask, strain, rdiag, cscale, dinv, weights, aff,
    vcls, ridx, inv, last, prev, ccol, cvol,
):
    start = jnp.int32(0)
    seen = [jnp.int32(0)] * 4
    for v in range(8):
        nb = vols[0, v]
        half = jnp.int32(0)
        for c in range(4):
            half = jnp.where(nb == c + 1, seen[c], half)
            seen[c] = seen[c] + jnp.where(nb == c + 1, 1, 0)
        vcls[(nb - 1) * 2 + half] = v
        for a in range(4):
            slot = (nb - 1) * nb + half * nb + a

            @pl.when(a < nb)
            def _():
                ridx[slot] = start + a
                inv[start + a] = slot
                last[slot] = 0

        cvol_id = (nb - 1) * 2 + half
        start = start + nb
        for a in range(4):
            pass
        vcls[8 + v] = cvol_id
    for c in range(4):
        for h in range(2):
            for a in range(c + 1):
                vcls[16 + static_row(c, h, a)] = c * 2 + h

    def link(c, carry):
        row = inv[off_row[c, 0]]
        ccol[c] = inv[off_col[c, 0]]
        cvol[c] = vcls[16 + row]
        prev[c] = last[row]
        last[row] = c + 1
        return carry

    lax.fori_loop(0, OFF, link, 0)

    lanes6 = iota((36, 128), 1)
    rows6 = iota((36, 128), 0)
    place = jnp.where(
        lanes6 == lax.rem(rows6, 6) * 8 + rows6 // 6, 1.0, 0.0
    ).astype(F32)
    aff[...] = lax.dot_general(
        affine[0], place, (((1,), (0,)), ((), ())),
        preferred_element_type=F32, precision=lax.Precision.HIGHEST,
    )
    eye = iota((128, 128), 0) == iota((128, 128), 1)

    def prepare(i, carry):
        r = ridx[i]
        values = jnp.where(eye, diag[r].astype(F32), 0.0)
        dinv[i] = 1.0 / jnp.sum(values, axis=0, keepdims=True)
        load = coupling[r]
        high = load.astype(BF16).astype(F32)
        block = jnp.zeros((58, 128), F32)
        weights[i] = jnp.concatenate([high, block, load - high, block], axis=0).astype(BF16)
        return carry

    lax.fori_loop(0, ROWS, prepare, 0)
    chain[0] = jnp.zeros((192, 128), F32)
    live = off_count[0]

    def phase(p, carry):
        def widen(i, c2):
            stage[pl.ds(pl.multiple_of(i * MSG, MSG), MSG), :] = got[2 * i + p].astype(F32)
            return c2

        lax.fori_loop(0, 64, widen, 0, unroll=2)
        tail = [stage[pl.ds(60 + k, 64, stride=MSG), :] for k in range(4)]
        for c in range(4):
            for h in range(2):
                v = vcls[c * 2 + h].astype(F32)
                picked = jnp.zeros((32, 128), F32)
                for k in range(4):
                    part = tail[k][h * 32 : (h + 1) * 32]
                    m = jnp.where(jnp.broadcast_to(part[:, 8:9], (32, 128)) == v, 1.0, 0.0)
                    mask[(c * 2 + h) * 4 + k] = m
                    picked = picked + m * part
                for i in range(6):
                    strain[(c * 2 + h) * 6 + i] = jnp.broadcast_to(picked[:, i : i + 1], (32, 128))
        for h in range(2):
            for a in range(4):
                for j in range(6):
                    sums = {}
                    for k in range(a, 4):
                        part = stage[pl.ds(h * 32 * MSG + BASE[k] + a * 6 + j, 32, stride=MSG), :]
                        for c in range(a, 4):
                            term = mask[(c * 2 + h) * 4 + k] * part
                            sums[c] = sums[c] + term if c in sums else term
                    for c in range(a, 4):
                        i = static_row(c, h, a)
                        state[i, j * 32 : (j + 1) * 32, :] = sums[c]
                        low[i, j * 32 : (j + 1) * 32, :] = sums[c].astype(BF16)

        def row_scale(i, c2):
            r = ridx[i]
            ch = vcls[16 + i]
            z = diag_n[r, 0, 0] * strain[ch * 6]
            for k in range(1, 6):
                z = z + diag_n[r, 0, k] * strain[ch * 6 + k]
            rdiag[i] = 1.0 / (1.0 + 0.4 * jnp.tanh(z))
            return c2

        lax.fori_loop(0, ROWS, row_scale, 0, unroll=4)

        def contact_scale(c, c2):
            ch = cvol[c]
            z = off_n[c, 0, 0] * strain[ch * 6]
            for k in range(1, 6):
                z = z + off_n[c, 0, k] * strain[ch * 6 + k]
            on = jnp.where(c < live, 1.0, 0.0).astype(F32)
            cscale[c] = (1.0 + 0.4 * jnp.tanh(z)) * on
            return c2

        lax.fori_loop(0, OFF, contact_scale, 0, unroll=4)

        def sweep(n, c2):
            def contact(c, c3):
                value = dot_nt(low[ccol[c]], off[c]).reshape(6, 32, 128)
                scaled = (value * cscale[c][None]).reshape(192, 128)
                chain[c + 1] = chain[prev[c]] + scaled
                return c3

            lax.fori_loop(0, OFF, contact, 0, unroll=4)

            def update(i, c3):
                r = ridx[i]
                own = dot_nt(low[i], diag[r]).reshape(6, 32, 128)
                extra = chain[last[i]].reshape(6, 32, 128)
                step = ((coupling[r][:, None, :] - extra) * rdiag[i][None] - own) * dinv[i][None]
                new = state[i] + step.reshape(192, 128)
                state[i] = new
                low[i] = new.astype(BF16)
                return c3

            lax.fori_loop(0, ROWS, update, 0, unroll=4)
            return c2

        lax.fori_loop(0, SWEEPS, sweep, 0)

        lane = iota((32, 128), 1)
        for c in range(4):
            for h in range(2):
                acc = jnp.zeros((192, 128), F32)
                for a in range(c + 1):
                    i = static_row(c, h, a)
                    x = state[i]
                    high = low[i]
                    acc = acc + dot_nt(high, weights[i])
                    acc = acc + dot_nt((x - high.astype(F32)).astype(BF16), weights[i])
                    for j in range(6):
                        stage[pl.ds(h * 32 * MSG + BASE[c] + a * 6 + j, 32, stride=MSG), :] = x[
                            j * 32 : (j + 1) * 32
                        ]
                t = acc[0:32]
                for j in range(1, 6):
                    t = t + pltpu.roll(acc[j * 32 : (j + 1) * 32], 8 * j, axis=1)
                t = t + pltpu.roll(t, 64, axis=1)
                v = vcls[c * 2 + h]
                tangent = aff[pl.ds(v, 1), :] - t / (128.0 * (c + 1))
                row = jnp.where(lane < 48, tangent, jnp.where(lane == 64, v.astype(F32), 0.0))
                stage[pl.ds(h * 32 * MSG + 60 + c, 32, stride=MSG), :] = row

        def lower(i, c2):
            back[2 * i + p] = stage[pl.ds(pl.multiple_of(i * MSG, MSG), MSG), :].astype(BF16)
            return c2

        lax.fori_loop(0, 64, lower, 0, unroll=2)
        return carry

    lax.fori_loop(0, 2, phase, 0)


def forces_of(grads_ref, s):
    g = [[grads_ref[3 * a + k : 3 * a + k + 1, :] for k in range(3)] for a in range(4)]
    out = []
    for a in range(4):
        gx, gy, gz = g[a]
        out.append(
            (
                gx * s[0] + gz * s[4] + gy * s[5],
                gy * s[1] + gz * s[3] + gx * s[5],
                gz * s[2] + gy * s[3] + gx * s[4],
            )
        )
    return out


def assemble(grads_ref, conn_ref, stress, scratch):
    forces = forces_of(grads_ref, stress)
    total = jnp.zeros((8, NODE), F32)
    for a in range(4):
        scratch[...] = jnp.zeros_like(scratch)
        for k in range(3):
            f = forces[a][k]
            high = f.astype(BF16).astype(F32)
            rest = f - high
            middle = rest.astype(BF16).astype(F32)
            scratch[k : k + 1, :] = high
            scratch[8 + k : 9 + k, :] = middle
            scratch[16 + k : 17 + k, :] = rest - middle
        part = dot_nt(scratch[...].astype(BF16), node_onehot(conn_ref, a))
        total = total + (part[0:8] + part[8:16] + part[16:24])
    return total[0:3]


def apply_tangent(tangent, strain, weight):
    acc = tangent[0:8] * strain[0]
    for j in range(1, 6):
        acc = acc + tangent[8 * j : 8 * j + 8] * strain[j]
    acc = acc * weight
    return [acc[i : i + 1, :] for i in range(6)]


def home_kernel(
    send, disp, load_ref, conn, grads, volume_ref, pmap,
    tail, body, residual_ref, product_ref, update_ref,
    tails, wide, small, small_e, mine, norms,
    own_sems, tail_send, tail_recv, body_send, body_recv, norm_send, norm_recv,
):
    sec, bulk, me = my_position()
    barrier = pltpu.get_barrier_semaphore()
    greet_all(barrier, sec, bulk)
    own_tail = pltpu.make_async_copy(send.at[me, pl.ds(48, 16)], tails.at[me], own_sems.at[0])
    own_body = pltpu.make_async_copy(send.at[me, pl.ds(0, 48)], body.at[me], own_sems.at[1])
    own_tail.start()
    own_body.start()
    pl.semaphore_wait(barrier, N_DEV - 1)

    def push_tail(step, carry):
        ty, tb, t = peer_of(step, sec, bulk)
        pltpu.make_async_remote_copy(
            src_ref=send.at[t, pl.ds(48, 16)],
            dst_ref=tails.at[me],
            send_sem=tail_send,
            recv_sem=tail_recv,
            device_id=(ty, tb),
            device_id_type=MESH,
        ).start()
        return carry

    def push_body(step, carry):
        ty, tb, t = peer_of(step, sec, bulk)
        pltpu.make_async_remote_copy(
            src_ref=send.at[t, pl.ds(0, 48)],
            dst_ref=body.at[me],
            send_sem=body_send,
            recv_sem=body_recv,
            device_id=(ty, tb),
            device_id_type=MESH,
        ).start()
        return carry

    lax.fori_loop(1, N_DEV, push_tail, 0)
    lax.fori_loop(1, N_DEV, push_body, 0)

    strain = strain_rows(gather_nodes(disp[...], conn, small), grads)
    where_to = pmap[...]
    owner = where_to // ELEM
    volume = (lax.rem(where_to, ELEM) // 64).astype(F32)
    same_owner = iota((N_DEV, ELEM), 0) == owner

    own_tail.wait()
    landed = tails.at[pl.ds(0, N_DEV - 1)]
    pltpu.make_async_copy(landed, landed, tail_recv).wait()
    wide[...] = tails[...].astype(F32).reshape(N_DEV * 16, 128)
    keep = pltpu.make_async_copy(tails, tail, own_sems.at[2])
    keep.start()
    tangent = jnp.zeros((128, ELEM), F32)
    for c in range(4):
        part = wide[pl.ds(12 + c, N_DEV, stride=16), :]
        code = jnp.broadcast_to(part[:, 64:65], (N_DEV, ELEM))
        pick = jnp.where(same_owner & (code == volume), 1.0, 0.0).astype(BF16)
        tangent = tangent + dot_nn(jnp.transpose(part).astype(BF16), pick)
    weight = volume_ref[...]
    residual = (
        assemble(grads, conn, apply_tangent(tangent, strain, weight), small_e) - load_ref[...]
    )
    residual_ref[...] = residual
    mine[...] = jnp.broadcast_to(
        jnp.sum(jnp.sum(residual * residual, axis=1, keepdims=True), axis=0, keepdims=True),
        (8, 128),
    )
    norms[me] = mine[...]

    def push_norm(step, carry):
        ty, tb, t = peer_of(step, sec, bulk)
        pltpu.make_async_remote_copy(
            src_ref=mine,
            dst_ref=norms.at[me],
            send_sem=norm_send,
            recv_sem=norm_recv,
            device_id=(ty, tb),
            device_id_type=MESH,
        ).start()
        return carry

    lax.fori_loop(1, N_DEV, push_norm, 0)
    trial = strain_rows(gather_nodes(residual, conn, small), grads)
    product_ref[...] = assemble(grads, conn, apply_tangent(tangent, trial, weight), small_e)
    arrived = norms.at[pl.ds(0, N_DEV - 1)]
    pltpu.make_async_copy(arrived, arrived, norm_recv).wait()
    total = jnp.sum(norms[...], axis=0)[0:1, :]
    root = jnp.sqrt(total / (3.0 * 16384) + 1e-06)
    update_ref[...] = -jnp.minimum(1.0, 1.0 / root) * residual

    pltpu.make_async_copy(arrived, arrived, norm_send).wait()
    keep.wait()
    own_body.wait()
    pltpu.make_async_copy(landed, landed, tail_send).wait()
    rest = body.at[pl.ds(0, N_DEV - 1)]
    pltpu.make_async_copy(rest, rest, body_send).wait()
    pltpu.make_async_copy(rest, rest, body_recv).wait()


def unpack_kernel(tail, body, pmap, out_hbm, stage, spread, flat, result, sems):
    make_spread(spread)

    def widen(i, carry):
        at = pl.multiple_of(i * MSG, MSG)
        stage[pl.ds(at, 48), :] = body[i].astype(F32)
        stage[pl.ds(at + 48, 16), :] = tail[i].astype(F32)
        return carry

    lax.fori_loop(0, N_DEV, widen, 0, unroll=2)
    where_to = pmap[...].astype(F32)
    column = jnp.transpose(jnp.broadcast_to(where_to, (128, ELEM))).astype(I32)
    owner = column // ELEM
    volume = lax.rem(column, ELEM) // 64
    same_owner = iota((ELEM, N_DEV), 1) == owner
    picks = []
    for c in range(4):
        part = stage[pl.ds(60 + c, N_DEV, stride=MSG), :]
        code = jnp.transpose(part)[64:65, :].astype(I32)
        picks.append(jnp.where(same_owner & (code == volume), 1.0, 0.0).astype(BF16))
    pick = jnp.concatenate(picks, axis=1)
    copies = []
    for a in range(4):
        for c in range(a, 4):
            row = jnp.concatenate(
                [
                    stage[pl.ds(BASE[c] + a * 6 + j, N_DEV, stride=MSG), :].astype(BF16)
                    for j in range(6)
                ],
                axis=1,
            )
            flat[c * 128 : (c + 1) * 128, :] = dot_nt(row, spread[...]).astype(BF16)
        result[:, a * LEVEL : (a + 1) * LEVEL] = dot_nn(
            pick[:, a * 128 :], flat[a * 128 :, :]
        ).astype(BF16)
        part = pl.ds(a * LEVEL, LEVEL)
        copy = pltpu.make_async_copy(result.at[:, part], out_hbm.at[:, part], sems.at[a])
        copy.start()
        copies.append(copy)
    for copy in copies:
        copy.wait()


VMEM = pl.BlockSpec(memory_space=pltpu.VMEM)
SMEM = pl.BlockSpec(memory_space=pltpu.SMEM)
ANY = pl.BlockSpec(memory_space=pl.ANY)
DMA = pltpu.SemaphoreType.DMA


def params(collective_id=None, limit=48):
    return pltpu.CompilerParams(
        collective_id=collective_id,
        has_side_effects=collective_id is not None,
        vmem_limit_bytes=limit * 2**20,
    )


def on_device(
    displacement, nodal_load, connectivity, shape_grads, elem_volume, point_map, vol_blocks,
    c_affine, coupling, diag_blocks, diag_normal, off_blocks, off_row, off_col, off_normal,
    off_count, fluct_state,
):
    pmap = point_map.reshape(1, ELEM)
    volume = elem_volume.reshape(1, ELEM)
    got = pl.pallas_call(
        pack_kernel,
        out_shape=jax.ShapeDtypeStruct((N_DEV, MSG, 128), BF16),
        in_specs=[VMEM, VMEM, VMEM, VMEM, ANY],
        out_specs=ANY,
        scratch_shapes=[
            pltpu.VMEM((ELEM, 4 * LEVEL), BF16),
            pltpu.VMEM((N_DEV * MSG, 128), F32),
            pltpu.VMEM((N_DEV, MSG, 128), BF16),
            pltpu.VMEM((LEVEL, LEVEL), BF16),
            pltpu.VMEM((128, ELEM), F32),
            pltpu.VMEM((32, 128), F32),
            DMA, DMA, DMA, DMA,
        ],
        compiler_params=params(1),
        name="pack",
    )(displacement, connectivity, shape_grads, pmap, fluct_state)
    smem = lambda n: pltpu.SMEM((n,), I32)
    back = pl.pallas_call(
        solve_kernel,
        out_shape=jax.ShapeDtypeStruct((N_DEV, MSG, 128), BF16),
        in_specs=[VMEM, SMEM, VMEM, VMEM, VMEM, SMEM, SMEM, SMEM, SMEM, SMEM, VMEM],
        out_specs=VMEM,
        scratch_shapes=[
            pltpu.VMEM((64 * MSG, 128), F32),
            pltpu.VMEM((ROWS, 192, 128), F32),
            pltpu.VMEM((ROWS, 192, 128), BF16),
            pltpu.VMEM((OFF + 1, 192, 128), F32),
            pltpu.VMEM((32, 32, 128), F32),
            pltpu.VMEM((48, 32, 128), F32),
            pltpu.VMEM((ROWS, 32, 128), F32),
            pltpu.VMEM((OFF, 32, 128), F32),
            pltpu.VMEM((ROWS, 1, 128), F32),
            pltpu.VMEM((ROWS, 128, 128), BF16),
            pltpu.VMEM((8, 128), F32),
            smem(36), smem(ROWS), smem(ROWS), smem(ROWS), smem(OFF), smem(OFF), smem(OFF),
        ],
        compiler_params=params(),
        name="solve",
    )(
        got, vol_blocks, coupling[:, 0], diag_blocks[:, 0], off_blocks[:, 0], diag_normal,
        off_normal, off_row, off_col, off_count, c_affine,
    )
    nodal = jax.ShapeDtypeStruct((3, NODE), F32)
    tail, body, residual, product, update = pl.pallas_call(
        home_kernel,
        out_shape=(
            jax.ShapeDtypeStruct((N_DEV, 16, 128), BF16),
            jax.ShapeDtypeStruct((N_DEV, 48, 128), BF16),
            nodal, nodal, nodal,
        ),
        in_specs=[VMEM] * 7,
        out_specs=(ANY, ANY, VMEM, VMEM, VMEM),
        scratch_shapes=[
            pltpu.VMEM((N_DEV, 16, 128), BF16),
            pltpu.VMEM((N_DEV * 16, 128), F32),
            pltpu.VMEM((32, 128), F32),
            pltpu.VMEM((32, ELEM), F32),
            pltpu.VMEM((8, 128), F32),
            pltpu.VMEM((N_DEV, 8, 128), F32),
            pltpu.SemaphoreType.DMA((3,)),
            DMA, DMA, DMA, DMA, DMA, DMA,
        ],
        compiler_params=params(2),
        name="home",
    )(back, displacement, nodal_load, connectivity, shape_grads, volume, pmap)
    fluct_new = pl.pallas_call(
        unpack_kernel,
        out_shape=jax.ShapeDtypeStruct((ELEM, 4 * LEVEL), BF16),
        in_specs=[VMEM, VMEM, VMEM],
        out_specs=ANY,
        scratch_shapes=[
            pltpu.VMEM((N_DEV * MSG, 128), F32),
            pltpu.VMEM((LEVEL, LEVEL), BF16),
            pltpu.VMEM((512, LEVEL), BF16),
            pltpu.VMEM((ELEM, 4 * LEVEL), BF16),
            pltpu.SemaphoreType.DMA((4,)),
        ],
        compiler_params=params(),
        name="unpack",
    )(tail, body, pmap)
    return residual, product, update, fluct_new


def solution(mesh):
    both = ("sec", "bulk")
    return jax.shard_map(
        on_device,
        mesh=mesh,
        in_specs=(
            P(None, both), P(None, both), P(None, both), P(None, both), P(both), P(both),
            P("bulk", None), P("bulk", None, None), P(None, "bulk", None, None),
            P(None, "bulk", None, None), P(None, "bulk", None), P(None, "bulk", None, None),
            P(None, "bulk"), P(None, "bulk"), P(None, "bulk", None), P("bulk"), P(both, None),
        ),
        out_specs=(P(None, both), P(None, both), P(None, both), P(both, None)),
        check_vma=False,
    )
```

time: 665 us -> 142 us (0.21); the launches traced: 653 us -> 141 us
  other arithmetic: 253 us -> 0 us
  local copies, waits for them, and re-layouts: 249 us -> 10.3 us
  Pallas kernels: 0 us -> 130 us
  blocking collectives: 67.1 us -> 0 us
  starting transfers between devices: 37.6 us -> 0 us
  matrix products: 30.9 us -> 0 us
  waiting for transfers between devices: 12.5 us -> 0 us
    scatter-add x9 -> x0, other arithmetic: 137 us -> none  [the longest x6 89.4 us: assemble(): jax.ops.segment_sum(forces[component].reshape(-1), flat_ids, num_segments...]
    pallas_call x0 -> x4, Pallas kernels: none -> 130 us  [the longest x1 46.8 us: on_device(): pl.pallas_call(pack_kernel, out_shape=jax.ShapeDtypeStruct((N_DEV, MSG, 1...]
    all_to_all x6 -> x0, other arithmetic: 76.9 us -> none  [the longest x2 39 us: on_device(): lax.all_to_all(state_send, ('sec', 'bulk'), split_axis=0, concat_axis=0,...]
    gather x20 -> x0, local copies, waits for them, and re-layouts: 67.3 us -> none  [the longest x3 11.7 us: contact_terms(): fluct_low[off_cols]]
    psum x1 -> x0, blocking collectives: 67.1 us -> none  [on_device(): norm_sq = lax.psum(jnp.sum(residual * residual), ('sec', 'bulk'))]
    mul x11 -> x0, local copies, waits for them, and re-layouts: 40.1 us -> none  [the longest x5 21.6 us: contact_terms(): result = applied.at[off_rows].add(contrib * off_scale_cols[:, None, :])]
    all_to_all x4 -> x0, starting transfers between devices: 37.6 us -> none  [the longest x1 11.5 us: on_device(): lax.all_to_all(strain_send, ('sec', 'bulk'), split_axis=0, concat_axis=0,...]
    all_to_all x4 -> x0, local copies, waits for them, and re-layouts: 34.4 us -> none  [the longest x2 17 us: on_device(): lax.all_to_all(state_send, ('sec', 'bulk'), split_axis=0, concat_axis=0,...]
  transfers between devices with their start and end apart: 4 -> 0, of which waited for: 1 -> 0; matrix products, arithmetic and copies ran while one was open for 36% -> 0% of each run, Pallas kernels for 0% -> 0%
where the time goes in v1:
time: 142 us; the launch traced here: 141 us
  Pallas kernels  130 us (92%)
  local copies, waits for them, and re-layouts  10.3 us (7%)
    pallas_call x1, Pallas kernels, on_device(): pl.pallas_call(pack_kernel, out_shape=jax.ShapeDtypeStruct((N_DEV, MSG, 1...  46.8 us
    pallas_call x1, Pallas kernels, on_device(): pl.pallas_call(home_kernel, out_shape=(jax.ShapeDtypeStruct((N_DEV, 16, 1...  42.1 us
    pallas_call x1, Pallas kernels, on_device(): pl.pallas_call(solve_kernel, out_shape=jax.ShapeDtypeStruct((N_DEV, MSG,...  33.2 us
    unnamed x29, local copies, waits for them, and re-layouts  9.48 us
    pallas_call x1, Pallas kernels, on_device(): pl.pallas_call(unpack_kernel, out_shape=jax.ShapeDtypeStruct((ELEM, 4 * L...  7.5 us

profile of v1, /device:TPU:1, one launch (start us, length us, event | category | flops | bytes accessed | tf_op | source)
XLA Modules:
  0.0 141.3 jit_solution(17324816878001189219)
XLA Ops:
  1.3 0.8 copy.27.diag_n
  2.1 0.7 copy.29.off_row
  2.8 0.7 copy.30.off_col
  3.5 0.8 copy.28.off_n
  4.3 0.8 copy.33
  5.1 0.0 copy-start
  5.1 1.9 %copy-done = bf16[512,3072]{1,0:T(8,128)(2,1)S(1)} copy-done((bf16[512,3072]{1,0:T(8,128)(2,1)S(1)}, bf16[512,3072]{1,0:T(8,128)(2,1)}, u32[]{:S(2)}) %copy-start) | copy-done | bytes 3145752
  7.0 0.0 copy-start.3
  7.0 0.8 copy-done.3
  7.8 0.0 copy-start.4
  7.8 0.7 copy-done.4
  8.5 0.0 copy-start.5
  8.5 0.7 copy-done.5
  9.2 0.0 copy-start.6
  9.2 0.7 copy-done.6
  9.8 0.0 copy-start.1
  9.8 0.0 copy-start.2
  9.8 0.0 copy-start.7
  9.8 0.0 copy-start.10
  9.8 46.8 %pack.1.got = bf16[128,64,128]{2,1,0:T(8,128)(2,1)S(1)} custom-call(f32[3,128]{1,0:T(4,128)S(1)} %copy-done.6, s32[4,512]{1,0:T(4,128)S(1)} %copy-done.4, f32[12,512]{1,0:T(8,128)S(1)} %copy-done.3, s32[1,512]{1,0:T(1,128)S(1)} %bitcast.11, bf16[512,3072]{1,0:T(8,128)(2,1)S(1)} %copy-done), custom_call_target="tpu_custom_call" | custom-call | tf_op jit(solution)/shard_map/pack/pallas_call | solution.py:584
  56.6 0.0 copy-done.1
  56.6 0.0 copy-done.2
  56.6 0.0 copy-done.7
  56.7 0.0 copy-done.10
  56.7 0.0 copy-start.8
  56.7 0.0 copy-start.9
  56.7 33.2 %solve.1.send = bf16[128,64,128]{2,1,0:T(8,128)(2,1)S(1)} custom-call(bf16[128,64,128]{2,1,0:T(8,128)(2,1)S(1)} %pack.1.got, s32[1,8]{1,0:T(1,128)S(1)} %copy-done.10, f32[20,6,128]{2,1,0:T(8,128)S(1)} %bitcast.10, bf16[20,128,128]{2,1,0:T(8,128)(2,1)S(1)} %bitcast.9, bf16[32,128,128]{2,1,0:T(8,128)(2,1)S(1)} %bitcast.8, f32[20,1,6]{2,1,0:T(1,128)S(1)} %copy.27.diag_n, ...), custom_call_target="tpu_custom_call" | custom-call | tf_op jit(solution)/shard_map/solve/pallas_call | solution.py:602
  89.9 0.0 copy-done.8
  89.9 0.0 copy-done.9
  89.9 42.1 %home.1 = (bf16[128,16,128]{2,1,0:T(8,128)(2,1)S(1)}, bf16[128,48,128]{2,1,0:T(8,128)(2,1)S(1)}, f32[3,128]{1,0:T(4,128)S(1)}, f32[3,128]{1,0:T(4,128)S(1)}, f32[3,128]{1,0:T(4,128)S(1)}) custom-call(bf16[128,64,128]{2,1,0:T(8,128)(2,1)S(1)} %solve.1.send, f32[3,128]{1,0:T(4,128)S(1)} %copy-done.6, f32[3,128]{1,0:T(4,128)S(1)} %copy-done.8, ...), custom_call_target="tpu_custom_call" | custom-call | tf_op jit(solution)/shard_map/home/pallas_call | solution.py:628
  132.1 7.5 %unpack.1 = bf16[512,3072]{1,0:T(8,128)(2,1)} custom-call(bf16[128,16,128]{2,1,0:T(8,128)(2,1)S(1)} %get-tuple-element.12.tail, bf16[128,48,128]{2,1,0:T(8,128)(2,1)S(1)} %get-tuple-element.13.body, s32[1,512]{1,0:T(1,128)S(1)} %bitcast.13), custom_call_target="tpu_custom_call" | custom-call | tf_op jit(solution)/shard_map/unpack/pallas_call | solution.py:650
  139.6 0.6 copy.38
  140.2 0.6 copy.39
  140.7 0.6 copy.40
Async XLA Ops:
  5.1 1.9 %copy-start = (bf16[512,3072]{1,0:T(8,128)(2,1)S(1)}, bf16[512,3072]{1,0:T(8,128)(2,1)}, u32[]{:S(2)}) copy-start(bf16[512,3072]{1,0:T(8,128)(2,1)} %state_hbm.1) | copy-start | bytes 9437188
  7.0 0.8 copy-start.3
  7.8 0.7 copy-start.4
  8.5 0.7 copy-start.5
  9.2 0.7 copy-start.6
  9.8 46.8 %copy-start.1 = (bf16[32,1,128,128]{3,2,1,0:T(8,128)(2,1)S(1)}, bf16[32,1,128,128]{3,2,1,0:T(8,128)(2,1)}, u32[]{:S(2)}) copy-start(bf16[32,1,128,128]{3,2,1,0:T(8,128)(2,1)} %param.28) | copy-start | bytes 3145732
  9.8 46.8 %copy-start.2 = (bf16[20,1,128,128]{3,2,1,0:T(8,128)(2,1)S(1)}, bf16[20,1,128,128]{3,2,1,0:T(8,128)(2,1)}, u32[]{:S(2)}) copy-start(bf16[20,1,128,128]{3,2,1,0:T(8,128)(2,1)} %param.26) | copy-start | bytes 1966084
  9.8 46.8 %copy-start.7 = (f32[1,8,36]{2,1,0:T(8,128)S(1)}, f32[1,8,36]{2,1,0:T(8,128)}, u32[]{:S(2)}) copy-start(f32[1,8,36]{2,1,0:T(8,128)} %affine.1) | copy-start | bytes 3460
  9.8 46.8 %copy-start.10 = (s32[1,8]{1,0:T(1,128)S(1)}, s32[1,8]{1,0:T(1,128)}, u32[]{:S(2)}) copy-start(s32[1,8]{1,0:T(1,128)} %vols.1) | copy-start | bytes 100
  56.7 33.3 %copy-start.8 = (f32[3,128]{1,0:T(4,128)S(1)}, f32[3,128]{1,0:T(4,128)}, u32[]{:S(2)}) copy-start(f32[3,128]{1,0:T(4,128)} %load_ref.1) | copy-start | bytes 4612
  56.7 33.3 %copy-start.9 = (f32[512]{0:T(512)S(1)}, f32[512]{0:T(512)}, u32[]{:S(2)}) copy-start(f32[512]{0:T(512)} %param.21) | copy-start | bytes 6148

commit v2 on v1

v2 whole, which is shorter than its diff:
```python
import jax
import jax.numpy as jnp
from jax import lax
from jax.experimental import pallas as pl
from jax.experimental.pallas import tpu as pltpu
from jax.sharding import PartitionSpec as P

F32 = jnp.float32
BF16 = jnp.bfloat16
I32 = jnp.int32
N_DEV = 128
ELEM = 512
NODE = 128
LEVEL = 768
MSG = 64
SWEEPS = 3
ROWS = 20
OFF = 32
MESH = pl.DeviceIdType.MESH
BASE = (0, 6, 18, 36)
SLOT0 = (0, 2, 6, 12)
STRIDE_PEER = 37
STRIDE_CHIP = 27
DELAY = True


def dot_nt(a, b):
    return lax.dot_general(a, b, (((1,), (1,)), ((), ())), preferred_element_type=F32)


def dot_nn(a, b):
    return lax.dot_general(a, b, (((1,), (0,)), ((), ())), preferred_element_type=F32)


def iota(shape, dim):
    return lax.broadcasted_iota(I32, shape, dim)


def static_row(c, h, a):
    return SLOT0[c] + h * (c + 1) + a


def my_position():
    sec = lax.axis_index("sec")
    bulk = lax.axis_index("bulk")
    return sec, bulk, sec * 32 + bulk


def peer_of(step, sec, bulk):
    d = lax.rem(step * STRIDE_PEER, N_DEV)
    ty = lax.rem(sec + d // 32, 4)
    tx = lax.rem(bulk // 8 + lax.rem(d // 8, 4), 4)
    tz = lax.rem(lax.rem(bulk // 2, 4) + lax.rem(d // 2, 4), 4)
    tc = lax.rem(lax.rem(bulk, 2) + lax.rem(d, 2), 2)
    tb = (tx * 4 + tz) * 2 + tc
    return ty, tb, ty * 32 + tb


def chip_peer(step, core, sec, bulk):
    d = lax.rem(step * STRIDE_CHIP, N_DEV // 2)
    ty = lax.rem(sec + d // 16, 4)
    tx = lax.rem(bulk // 8 + lax.rem(d // 4, 4), 4)
    tz = lax.rem(lax.rem(bulk // 2, 4) + lax.rem(d, 4), 4)
    tb = (tx * 4 + tz) * 2 + core
    return ty, tb, ty * 32 + tb


def greet_all(barrier, sec, bulk):
    def greet(step, carry):
        ty, tb, _ = peer_of(step, sec, bulk)
        pl.semaphore_signal(barrier, inc=1, device_id=(ty, tb), device_id_type=MESH)
        return carry

    lax.fori_loop(1, N_DEV, greet, 0)


def split3(nodal, scratch):
    high = nodal.astype(BF16).astype(F32)
    rest = nodal - high
    middle = rest.astype(BF16).astype(F32)
    low = rest - middle
    scratch[...] = jnp.zeros_like(scratch)
    rows = nodal.shape[0]
    scratch[0:rows, :] = high
    scratch[8 : 8 + rows, :] = middle
    scratch[16 : 16 + rows, :] = low
    return scratch[...].astype(BF16)


def node_onehot(conn_ref, a):
    ids = conn_ref[a : a + 1, :]
    return jnp.where(iota((NODE, ELEM), 0) == ids, 1.0, 0.0).astype(BF16)


def gather_nodes(nodal, conn_ref, scratch):
    parts = split3(nodal, scratch)
    out = []
    for a in range(4):
        got = dot_nn(parts, node_onehot(conn_ref, a))
        out.append(got[0:8] + got[8:16] + got[16:24])
    return out


def strain_rows(moved, grads_ref):
    g = [[grads_ref[3 * a + k : 3 * a + k + 1, :] for k in range(3)] for a in range(4)]
    u = [[moved[a][k : k + 1, :] for k in range(3)] for a in range(4)]

    def total(terms):
        out = terms[0]
        for t in terms[1:]:
            out = out + t
        return out

    return [
        total([g[a][0] * u[a][0] for a in range(4)]),
        total([g[a][1] * u[a][1] for a in range(4)]),
        total([g[a][2] * u[a][2] for a in range(4)]),
        total([g[a][2] * u[a][1] + g[a][1] * u[a][2] for a in range(4)]),
        total([g[a][2] * u[a][0] + g[a][0] * u[a][2] for a in range(4)]),
        total([g[a][1] * u[a][0] + g[a][0] * u[a][1] for a in range(4)]),
    ]


def make_spread(spread):
    n = iota((1, LEVEL), 1)
    source = lax.rem(n, 128) * 6 + n // 128
    spread[...] = jnp.where(iota((LEVEL, LEVEL), 0) == source, 1.0, 0.0).astype(BF16)


def prepare_send(strain, pmap, state, stage, send, spread, flat, srows, load):
    srows[...] = jnp.zeros_like(srows)
    for i in range(6):
        srows[i : i + 1, :] = strain[i]
    where_to = pmap[...]
    owner = where_to // ELEM
    volume = lax.rem(where_to, ELEM) // 64
    srows[8:9, :] = volume.astype(F32)
    strain_low = srows[...].astype(BF16)
    make_spread(spread)
    load.wait()

    ones = jnp.ones((16, LEVEL), BF16)
    levels = jnp.zeros((1, ELEM), I32)
    for a in range(4):
        weight = dot_nt(ones, jnp.abs(state[:, a * LEVEL : (a + 1) * LEVEL]))[0:1, :]
        levels = jnp.where(weight > 0.0, a + 1, levels)
    key = (owner * 4096 + levels * 512 + iota((1, ELEM), 1)).astype(F32)
    key_col = jnp.transpose(jnp.broadcast_to(key, (128, ELEM)))
    order = []
    for m in range(4):
        part = key[:, m * 128 : (m + 1) * 128]
        order.append(jnp.sum(jnp.where(key_col < part, 1.0, 0.0), axis=0, keepdims=True))
    order = jnp.concatenate(order, axis=1).astype(I32)

    at = 0
    for k in range(4):
        pick = jnp.where(order == iota((N_DEV, ELEM), 0) * 4 + k, 1.0, 0.0).astype(BF16)
        for a in range(k + 1):
            mine = dot_nn(pick, state[:, a * LEVEL : (a + 1) * LEVEL])
            flat[at * 128 : (at + 1) * 128, :] = mine.astype(BF16)
            at += 1
        stage[pl.ds(60 + k, N_DEV, stride=MSG), :] = dot_nt(pick, strain_low)
    for jj in range(3):
        for half in range(2):
            got = dot_nn(
                flat[half * 640 : (half + 1) * 640, :], spread[:, jj * 256 : (jj + 1) * 256]
            )
            for i in range(5):
                at = half * 5 + i
                for j in range(2):
                    stage[pl.ds(at * 6 + jj * 2 + j, N_DEV, stride=MSG), :] = got[
                        i * 128 : (i + 1) * 128, j * 128 : (j + 1) * 128
                    ]

    def lower(i, carry):
        at = pl.multiple_of(i * 2 * MSG, 2 * MSG)
        send[pl.ds(i * 2, 2)] = (
            stage[pl.ds(at, 2 * MSG), :].astype(BF16).reshape(2, MSG, 128)
        )
        return carry

    lax.fori_loop(0, N_DEV // 2, lower, 0, unroll=4)


def make_tables(vols, off_row, off_col, vcls, chrow, ridx, inv, last, prev, crow, ccol, cvol):
    sizes = [vols[0, v] for v in range(8)]
    zero = jnp.int32(0)
    halves, starts, start = [], [], zero
    for v in range(8):
        half = zero
        for w in range(v):
            half = half + jnp.where(sizes[w] == sizes[v], 1, 0)
        halves.append(half)
        starts.append(start)
        start = start + sizes[v]
    for c in range(4):
        for h in range(2):
            vol, first = zero, zero
            for v in range(8):
                hit = (sizes[v] == c + 1) & (halves[v] == h)
                vol = jnp.where(hit, v, vol)
                first = jnp.where(hit, starts[v], first)
            vcls[c * 2 + h] = vol
            for a in range(c + 1):
                ridx[static_row(c, h, a)] = first + a
                chrow[static_row(c, h, a)] = c * 2 + h

    def invert(r, carry):
        found = jnp.int32(0)
        for i in range(ROWS):
            found = jnp.where(ridx[i] == r, i, found)
        inv[r] = found
        return carry

    lax.fori_loop(0, ROWS, invert, 0)

    def ends(c, carry):
        row = inv[off_row[0, c]]
        crow[c] = row
        ccol[c] = inv[off_col[0, c]]
        cvol[c] = chrow[row]
        return carry

    lax.fori_loop(0, OFF, ends, 0)

    def link(c, carry):
        row = crow[c]
        before = jnp.int32(0)
        for k in range(OFF):
            before = jnp.where((crow[k] == row) & (k < c), k + 1, before)
        prev[c] = before
        return carry

    lax.fori_loop(0, OFF, link, 0)

    def finish(i, carry):
        end = jnp.int32(0)
        for k in range(OFF):
            end = jnp.where(crow[k] == i, k + 1, end)
        last[i] = end
        return carry

    lax.fori_loop(0, ROWS, finish, 0)


def step_kernel(
    disp, load_ref, conn, grads, volume_ref, pmap, vols, affine, diag_n, off_n, off_row,
    off_col, off_count, coupling_hbm, diag_hbm, off_hbm, state_hbm,
    tail, body, residual_ref, product_ref, update_ref,
    fluct, stage, send, spread, flat, srows, small, small_e,
    got, back, coupling, diag, off,
    state, low, chain, mask, strain, rdiag, cscale, dinv, weights, aff,
    tails, wide, mine, norms,
    vcls, chrow, ridx, inv, last, prev, crow, ccol, cvol,
    load_sems, own_sems, go_send, go_recv, tail_send, tail_recv, body_send, body_recv,
    norm_send, norm_recv,
):
    sec, bulk, me = my_position()
    core = lax.rem(bulk, 2)
    barrier = pltpu.get_barrier_semaphore()
    loads = []
    for i, (source, target) in enumerate(
        [(state_hbm, fluct), (off_hbm, off), (diag_hbm, diag), (coupling_hbm, coupling)]
    ):
        loads.append(pltpu.make_async_copy(source, target, load_sems.at[i]))
        loads[-1].start()
    greet_all(barrier, sec, bulk)
    macro = strain_rows(gather_nodes(disp[...], conn, small), grads)
    prepare_send(macro, pmap, fluct, stage, send, spread, flat, srows, loads[0])
    own = pltpu.make_async_copy(send.at[me], got.at[core, me // 2], own_sems.at[0])
    own.start()
    pl.semaphore_wait(barrier, N_DEV - 1)

    def push(step, carry):
        ty, tb, t = peer_of(step, sec, bulk)
        pltpu.make_async_remote_copy(
            src_ref=send.at[t],
            dst_ref=got.at[core, me // 2],
            send_sem=go_send,
            recv_sem=go_recv.at[core],
            device_id=(ty, tb),
            device_id_type=MESH,
        ).start()
        return carry

    if DELAY:

        @pl.when(core == 0)
        def _():
            lax.fori_loop(1, N_DEV, push, 0)

    else:
        lax.fori_loop(1, N_DEV, push, 0)

    make_tables(vols, off_row, off_col, vcls, chrow, ridx, inv, last, prev, crow, ccol, cvol)
    lanes6 = iota((36, 128), 1)
    rows6 = iota((36, 128), 0)
    place = jnp.where(lanes6 == lax.rem(rows6, 6) * 8 + rows6 // 6, 1.0, 0.0).astype(F32)
    spread_affine = lax.dot_general(
        affine[0], place, (((1,), (0,)), ((), ())),
        preferred_element_type=F32, precision=lax.Precision.HIGHEST,
    )
    for v in range(8):
        aff[v] = spread_affine[v : v + 1, :]
    eye = iota((128, 128), 0) == iota((128, 128), 1)
    for load in loads[1:]:
        load.wait()

    def prepare(i, carry):
        r = ridx[i]
        values = jnp.where(eye, diag[r].astype(F32), 0.0)
        dinv[i] = 1.0 / jnp.sum(values, axis=0, keepdims=True)
        load = coupling[r].reshape(6, 128)
        high = load.astype(BF16).astype(F32)
        block = jnp.zeros((58, 128), F32)
        weights[i] = jnp.concatenate([high, block, load - high, block], axis=0).astype(BF16)
        return carry

    lax.fori_loop(0, ROWS, prepare, 0, unroll=2)
    chain[0] = jnp.zeros((192, 128), F32)
    live = off_count[0]
    own.wait()

    def phase(p, carry):
        @pl.when(core == p)
        def _():
            part = got.at[p, pl.ds(0, 63)]
            pltpu.make_async_copy(part, part, go_recv.at[p]).wait()

        @pl.when(core != p)
        def _():
            part = got.at[p]
            pltpu.make_async_copy(part, part, go_recv.at[p]).wait()

        if DELAY:

            @pl.when((p == 0) & (core == 1))
            def _():
                lax.fori_loop(1, N_DEV, push, 0)

        def widen(i, c2):
            at = pl.multiple_of(i * 2 * MSG, 2 * MSG)
            stage[pl.ds(at, 2 * MSG), :] = (
                got[p, pl.ds(2 * i, 2)].astype(F32).reshape(2 * MSG, 128)
            )
            return c2

        lax.fori_loop(0, 32, widen, 0, unroll=4)
        rest = [stage[pl.ds(60 + k, 64, stride=MSG), :] for k in range(4)]
        for c in range(4):
            for h in range(2):
                v = vcls[c * 2 + h].astype(F32)
                picked = jnp.zeros((32, 128), F32)
                for k in range(4):
                    part = rest[k][h * 32 : (h + 1) * 32]
                    m = jnp.where(jnp.broadcast_to(part[:, 8:9], (32, 128)) == v, 1.0, 0.0)
                    mask[(c * 2 + h) * 4 + k] = m
                    picked = picked + m * part
                for i in range(6):
                    strain[(c * 2 + h) * 6 + i] = jnp.broadcast_to(picked[:, i : i + 1], (32, 128))
        for h in range(2):
            for a in range(4):
                for j in range(6):
                    sums = {}
                    for k in range(a, 4):
                        part = stage[pl.ds(h * 32 * MSG + BASE[k] + a * 6 + j, 32, stride=MSG), :]
                        for c in range(a, 4):
                            term = mask[(c * 2 + h) * 4 + k] * part
                            sums[c] = sums[c] + term if c in sums else term
                    for c in range(a, 4):
                        i = static_row(c, h, a)
                        state[i, j * 32 : (j + 1) * 32, :] = sums[c]
                        low[i, j * 32 : (j + 1) * 32, :] = sums[c].astype(BF16)

        def row_scale(i, c2):
            r = ridx[i]
            ch = chrow[i] * 6
            z = diag_n[0, 0, r] * strain[ch]
            for k in range(1, 6):
                z = z + diag_n[k, 0, r] * strain[ch + k]
            rdiag[i] = 1.0 / (1.0 + 0.4 * jnp.tanh(z))
            return c2

        lax.fori_loop(0, ROWS, row_scale, 0, unroll=5)

        def contact_scale(c, c2):
            ch = cvol[c] * 6
            z = off_n[0, 0, c] * strain[ch]
            for k in range(1, 6):
                z = z + off_n[k, 0, c] * strain[ch + k]
            on = jnp.where(c < live, 1.0, 0.0).astype(F32)
            cscale[c] = (1.0 + 0.4 * jnp.tanh(z)) * on
            return c2

        lax.fori_loop(0, OFF, contact_scale, 0, unroll=8)

        def sweep(n, c2):
            def contact(c, c3):
                value = dot_nt(low[ccol[c]], off[c]).reshape(6, 32, 128)
                scaled = (value * cscale[c][None]).reshape(192, 128)
                chain[c + 1] = chain[prev[c]] + scaled
                return c3

            lax.fori_loop(0, OFF, contact, 0, unroll=4)

            def update(i, c3):
                r = ridx[i]
                own_part = dot_nt(low[i], diag[r]).reshape(6, 32, 128)
                extra = chain[last[i]].reshape(6, 32, 128)
                step = ((coupling[r] - extra) * rdiag[i][None] - own_part) * dinv[i][None]
                new = state[i] + step.reshape(192, 128)
                state[i] = new
                low[i] = new.astype(BF16)
                return c3

            lax.fori_loop(0, ROWS, update, 0, unroll=4)
            return c2

        lax.fori_loop(0, SWEEPS, sweep, 0)

        lane = iota((32, 128), 1)
        for c in range(4):
            for h in range(2):
                acc = jnp.zeros((192, 128), F32)
                for a in range(c + 1):
                    i = static_row(c, h, a)
                    x = state[i]
                    high = low[i]
                    acc = acc + dot_nt(high, weights[i])
                    acc = acc + dot_nt((x - high.astype(F32)).astype(BF16), weights[i])
                    for j in range(6):
                        stage[pl.ds(h * 32 * MSG + BASE[c] + a * 6 + j, 32, stride=MSG), :] = x[
                            j * 32 : (j + 1) * 32
                        ]
                t = acc[0:32]
                for j in range(1, 6):
                    t = t + pltpu.roll(acc[j * 32 : (j + 1) * 32], 8 * j, axis=1)
                t = t + pltpu.roll(t, 64, axis=1)
                v = vcls[c * 2 + h]
                tangent = aff[v] - t / (128.0 * (c + 1))
                row = jnp.where(lane < 48, tangent, jnp.where(lane == 64, v.astype(F32), 0.0))
                stage[pl.ds(h * 32 * MSG + 60 + c, 32, stride=MSG), :] = row

        def lower(i, c2):
            at = pl.multiple_of(i * 2 * MSG, 2 * MSG)
            back[p, pl.ds(2 * i, 2)] = (
                stage[pl.ds(at, 2 * MSG), :].astype(BF16).reshape(2, MSG, 128)
            )
            return c2

        lax.fori_loop(0, 32, lower, 0, unroll=4)

        def push_tail(step, c2):
            ty, tb, t = chip_peer(step, p, sec, bulk)
            pltpu.make_async_remote_copy(
                src_ref=back.at[p, t // 2, pl.ds(48, 16)],
                dst_ref=tails.at[me],
                send_sem=tail_send,
                recv_sem=tail_recv,
                device_id=(ty, tb),
                device_id_type=MESH,
            ).start()
            return c2

        def push_body(step, c2):
            ty, tb, t = chip_peer(step, p, sec, bulk)
            pltpu.make_async_remote_copy(
                src_ref=back.at[p, t // 2, pl.ds(0, 48)],
                dst_ref=body.at[me],
                send_sem=body_send,
                recv_sem=body_recv,
                device_id=(ty, tb),
                device_id_type=MESH,
            ).start()
            return c2

        lax.fori_loop(1, N_DEV // 2, push_tail, 0)

        @pl.when(core != p)
        def _():
            push_tail(0, 0)

        lax.fori_loop(1, N_DEV // 2, push_body, 0)

        @pl.when(core != p)
        def _():
            push_body(0, 0)

        return carry

    lax.fori_loop(0, 2, phase, 0)
    mine_back = back.at[core, me // 2]
    own_tail = pltpu.make_async_copy(mine_back.at[pl.ds(48, 16)], tails.at[me], own_sems.at[0])
    own_body = pltpu.make_async_copy(mine_back.at[pl.ds(0, 48)], body.at[me], own_sems.at[1])
    own_tail.start()
    own_body.start()

    where_to = pmap[...]
    owner = where_to // ELEM
    volume = (lax.rem(where_to, ELEM) // 64).astype(F32)
    same_owner = iota((N_DEV, ELEM), 0) == owner
    own_tail.wait()
    landed = tails.at[pl.ds(0, N_DEV - 1)]
    pltpu.make_async_copy(landed, landed, tail_recv).wait()
    wide[...] = tails[...].astype(F32).reshape(N_DEV * 16, 128)
    keep = pltpu.make_async_copy(tails, tail, own_sems.at[2])
    keep.start()
    tangent = jnp.zeros((128, ELEM), F32)
    for c in range(4):
        part = wide[pl.ds(12 + c, N_DEV, stride=16), :]
        code = jnp.broadcast_to(part[:, 64:65], (N_DEV, ELEM))
        pick = jnp.where(same_owner & (code == volume), 1.0, 0.0).astype(BF16)
        tangent = tangent + dot_nn(jnp.transpose(part).astype(BF16), pick)
    weight = volume_ref[...]
    macro_rows = [srows[i : i + 1, :] for i in range(6)]
    residual = (
        assemble(grads, conn, apply_tangent(tangent, macro_rows, weight), small_e) - load_ref[...]
    )
    residual_ref[...] = residual
    mine[...] = jnp.broadcast_to(
        jnp.sum(jnp.sum(residual * residual, axis=1, keepdims=True), axis=0, keepdims=True),
        (8, 128),
    )
    norms[me] = mine[...]

    def push_norm(step, carry):
        ty, tb, t = peer_of(step, sec, bulk)
        pltpu.make_async_remote_copy(
            src_ref=mine,
            dst_ref=norms.at[me],
            send_sem=norm_send,
            recv_sem=norm_recv,
            device_id=(ty, tb),
            device_id_type=MESH,
        ).start()
        return carry

    lax.fori_loop(1, N_DEV, push_norm, 0)
    trial = strain_rows(gather_nodes(residual, conn, small), grads)
    product_ref[...] = assemble(grads, conn, apply_tangent(tangent, trial, weight), small_e)
    arrived = norms.at[pl.ds(0, N_DEV - 1)]
    pltpu.make_async_copy(arrived, arrived, norm_recv).wait()
    total = jnp.sum(norms[...], axis=0)[0:1, :]
    root = jnp.sqrt(total / (3.0 * 16384) + 1e-06)
    update_ref[...] = -jnp.minimum(1.0, 1.0 / root) * residual

    sent = send.at[pl.ds(0, N_DEV - 1)]
    pltpu.make_async_copy(sent, sent, go_send).wait()
    pltpu.make_async_copy(arrived, arrived, norm_send).wait()
    keep.wait()
    own_body.wait()
    pltpu.make_async_copy(landed, landed, tail_send).wait()
    rest = body.at[pl.ds(0, N_DEV - 1)]
    pltpu.make_async_copy(rest, rest, body_send).wait()
    pltpu.make_async_copy(rest, rest, body_recv).wait()


def unpack_kernel(
    residual, product, update, tail, body, pmap,
    out_residual, out_product, out_update, out_hbm,
    stage, spread, rows, flat, result, sems,
):
    out_residual[...] = residual[...]
    out_product[...] = product[...]
    out_update[...] = update[...]
    make_spread(spread)

    def widen(i, carry):
        at = pl.multiple_of(i * MSG, MSG)
        stage[pl.ds(at, 48), :] = body[i].astype(F32)
        stage[pl.ds(at + 48, 16), :] = tail[i].astype(F32)
        return carry

    lax.fori_loop(0, N_DEV, widen, 0, unroll=8)
    where_to = pmap[...].astype(F32)
    column = jnp.transpose(jnp.broadcast_to(where_to, (128, ELEM))).astype(I32)
    owner = column // ELEM
    volume = lax.rem(column, ELEM) // 64
    same_owner = iota((ELEM, N_DEV), 1) == owner
    picks = []
    for c in range(4):
        part = stage[pl.ds(60 + c, N_DEV, stride=MSG), :]
        code = jnp.transpose(part)[64:65, :].astype(I32)
        picks.append(jnp.where(same_owner & (code == volume), 1.0, 0.0).astype(BF16))
    pick = jnp.concatenate(picks, axis=1)
    copies = []
    for a in range(4):
        for c in range(a, 4):
            for j in range(6):
                rows[c * 128 : (c + 1) * 128, j * 128 : (j + 1) * 128] = stage[
                    pl.ds(BASE[c] + a * 6 + j, N_DEV, stride=MSG), :
                ].astype(BF16)
        flat[a * 128 :, :] = dot_nt(rows[a * 128 :, :], spread[...]).astype(BF16)
        result[:, a * LEVEL : (a + 1) * LEVEL] = dot_nn(
            pick[:, a * 128 :], flat[a * 128 :, :]
        ).astype(BF16)
        part = pl.ds(a * LEVEL, LEVEL)
        copy = pltpu.make_async_copy(result.at[:, part], out_hbm.at[:, part], sems.at[a])
        copy.start()
        copies.append(copy)
    for copy in copies:
        copy.wait()


def forces_of(grads_ref, s):
    g = [[grads_ref[3 * a + k : 3 * a + k + 1, :] for k in range(3)] for a in range(4)]
    out = []
    for a in range(4):
        gx, gy, gz = g[a]
        out.append(
            (
                gx * s[0] + gz * s[4] + gy * s[5],
                gy * s[1] + gz * s[3] + gx * s[5],
                gz * s[2] + gy * s[3] + gx * s[4],
            )
        )
    return out


def assemble(grads_ref, conn_ref, stress, scratch):
    forces = forces_of(grads_ref, stress)
    total = jnp.zeros((8, NODE), F32)
    for a in range(4):
        scratch[...] = jnp.zeros_like(scratch)
        for k in range(3):
            f = forces[a][k]
            high = f.astype(BF16).astype(F32)
            rest = f - high
            middle = rest.astype(BF16).astype(F32)
            scratch[k : k + 1, :] = high
            scratch[8 + k : 9 + k, :] = middle
            scratch[16 + k : 17 + k, :] = rest - middle
        part = dot_nt(scratch[...].astype(BF16), node_onehot(conn_ref, a))
        total = total + (part[0:8] + part[8:16] + part[16:24])
    return total[0:3]


def apply_tangent(tangent, strain, weight):
    acc = tangent[0:8] * strain[0]
    for j in range(1, 6):
        acc = acc + tangent[8 * j : 8 * j + 8] * strain[j]
    acc = acc * weight
    return [acc[i : i + 1, :] for i in range(6)]


VMEM = pl.BlockSpec(memory_space=pltpu.VMEM)
SMEM = pl.BlockSpec(memory_space=pltpu.SMEM)
ANY = pl.BlockSpec(memory_space=pl.ANY)
DMA = pltpu.SemaphoreType.DMA


def params(collective_id=None, limit=48):
    return pltpu.CompilerParams(
        collective_id=collective_id,
        has_side_effects=collective_id is not None,
        vmem_limit_bytes=limit * 2**20,
    )


def on_device(
    displacement, nodal_load, connectivity, shape_grads, elem_volume, point_map, vol_blocks,
    c_affine, coupling, diag_blocks, diag_normal, off_blocks, off_row, off_col, off_normal,
    off_count, fluct_state,
):
    pmap = point_map.reshape(1, ELEM)
    volume = elem_volume.reshape(1, ELEM)
    smem = lambda n: pltpu.SMEM((n,), I32)
    vmem = pltpu.VMEM
    nodal = jax.ShapeDtypeStruct((3, NODE), F32)
    tail, body, residual, product, update = pl.pallas_call(
        step_kernel,
        out_shape=(
            jax.ShapeDtypeStruct((N_DEV, 16, 128), BF16),
            jax.ShapeDtypeStruct((N_DEV, 48, 128), BF16),
            nodal, nodal, nodal,
        ),
        in_specs=[VMEM] * 6 + [SMEM, VMEM] + [SMEM] * 5 + [ANY] * 4,
        out_specs=(ANY, ANY, VMEM, VMEM, VMEM),
        scratch_shapes=[
            vmem((ELEM, 4 * LEVEL), BF16),
            vmem((N_DEV * MSG, 128), F32),
            vmem((N_DEV, MSG, 128), BF16),
            vmem((LEVEL, LEVEL), BF16),
            vmem((1280, LEVEL), BF16),
            vmem((128, ELEM), F32),
            vmem((32, 128), F32),
            vmem((32, ELEM), F32),
            vmem((2, 64, MSG, 128), BF16),
            vmem((2, 64, MSG, 128), BF16),
            vmem((ROWS, 6, 1, 128), F32),
            vmem((ROWS, 128, 128), BF16),
            vmem((OFF, 128, 128), BF16),
            vmem((ROWS, 192, 128), F32),
            vmem((ROWS, 192, 128), BF16),
            vmem((OFF + 1, 192, 128), F32),
            vmem((32, 32, 128), F32),
            vmem((48, 32, 128), F32),
            vmem((ROWS, 32, 128), F32),
            vmem((OFF, 32, 128), F32),
            vmem((ROWS, 1, 128), F32),
            vmem((ROWS, 128, 128), BF16),
            vmem((8, 1, 128), F32),
            vmem((N_DEV, 16, 128), BF16),
            vmem((N_DEV * 16, 128), F32),
            vmem((8, 128), F32),
            vmem((N_DEV, 8, 128), F32),
            smem(8), smem(ROWS), smem(ROWS), smem(ROWS), smem(ROWS),
            smem(OFF), smem(OFF), smem(OFF), smem(OFF),
            DMA((4,)), DMA((3,)), DMA, DMA((2,)), DMA, DMA, DMA, DMA, DMA, DMA,
        ],
        compiler_params=params(1, 60),
        name="step",
    )(
        displacement, nodal_load, connectivity, shape_grads, volume, pmap, vol_blocks, c_affine,
        diag_normal.transpose(2, 1, 0), off_normal.transpose(2, 1, 0), off_row.T, off_col.T,
        off_count, coupling.transpose(0, 2, 1, 3), diag_blocks[:, 0], off_blocks[:, 0],
        fluct_state,
    )
    return pl.pallas_call(
        unpack_kernel,
        out_shape=(nodal, nodal, nodal, jax.ShapeDtypeStruct((ELEM, 4 * LEVEL), BF16)),
        in_specs=[VMEM] * 6,
        out_specs=(VMEM, VMEM, VMEM, ANY),
        scratch_shapes=[
            vmem((N_DEV * MSG, 128), F32),
            vmem((LEVEL, LEVEL), BF16),
            vmem((512, LEVEL), BF16),
            vmem((512, LEVEL), BF16),
            vmem((ELEM, 4 * LEVEL), BF16),
            DMA((4,)),
        ],
        compiler_params=params(None, 60),
        name="unpack",
    )(residual, product, update, tail, body, pmap)


def solution(mesh):
    both = ("sec", "bulk")
    return jax.shard_map(
        on_device,
        mesh=mesh,
        in_specs=(
            P(None, both), P(None, both), P(None, both), P(None, both), P(both), P(both),
            P("bulk", None), P("bulk", None, None), P(None, "bulk", None, None),
            P(None, "bulk", None, None), P(None, "bulk", None), P(None, "bulk", None, None),
            P(None, "bulk"), P(None, "bulk"), P(None, "bulk", None), P("bulk"), P(both, None),
        ),
        out_specs=(P(None, both), P(None, both), P(None, both), P(both, None)),
        check_vma=False,
    )
```

time: 142 us -> 104 us (0.73)
  Pallas kernels: 130 us -> 103 us
  local copies, waits for them, and re-layouts: 10.3 us -> 0 us
    pallas_call x4 -> x2, Pallas kernels: 130 us -> 103 us  [the longest x1 93.7 us: on_device(): pl.pallas_call(step_kernel, out_shape=(jax.ShapeDtypeStruct((N_DEV, 16, 1...]
    unnamed x29 -> x0, local copies, waits for them, and re-layouts: 9.48 us -> none
where the time goes in v2:
time: 104 us
  Pallas kernels  103 us (99%)
  between operations  1.45 us (1%)
    pallas_call x1, Pallas kernels, on_device(): pl.pallas_call(step_kernel, out_shape=(jax.ShapeDtypeStruct((N_DEV, 16, 1...  93.7 us
    pallas_call x1, Pallas kernels, on_device(): pl.pallas_call(unpack_kernel, out_shape=(nodal, nodal, nodal, jax.ShapeDt...  8.98 us

profile of v2, /device:TPU:1, one launch (start us, length us, event | category | flops | bytes accessed | tf_op | source)
XLA Modules:
  0.0 104.1 jit_solution(733322616318056609)
XLA Ops:
  1.3 93.7 %step.1 = (bf16[128,16,128]{2,1,0:T(8,128)(2,1)}, bf16[128,48,128]{2,1,0:T(8,128)(2,1)}, f32[3,128]{1,0:T(4,128)}, f32[3,128]{1,0:T(4,128)}, f32[3,128]{1,0:T(4,128)}) custom-call(f32[3,128]{1,0:T(4,128)} %disp.1, f32[3,128]{1,0:T(4,128)} %load_ref.1, s32[4,512]{1,0:T(4,128)} %conn.1, f32[12,512]{1,0:T(8,128)} %grads.1, f32[1,512]{1,0:T(1,128)} %bitcast.16, ...), custom_call_target="tpu_custom_call" | custom-call | tf_op jit(solution)/shard_map/step/pallas_call | solution.py:670
  95.0 9.0 %unpack.1 = (f32[3,128]{1,0:T(4,128)}, f32[3,128]{1,0:T(4,128)}, f32[3,128]{1,0:T(4,128)}, bf16[512,3072]{1,0:T(8,128)(2,1)}) custom-call(f32[3,128]{1,0:T(4,128)} %get-tuple-element.9.residual, f32[3,128]{1,0:T(4,128)} %get-tuple-element.10.product, f32[3,128]{1,0:T(4,128)} %get-tuple-element.11.update, bf16[128,16,128]{2,1,0:T(8,128)(2,1)} %get-tuple-element.12.tail, ...), custom_call_target="tpu_custom_call" | custom-call | tf_op jit(solution)/shard_map/unpack/pallas_call | solution.py:719

commit v3 on v2

--- a/solution.py
+++ b/solution.py
@@ -19,9 +19,9 @@
 MESH = pl.DeviceIdType.MESH
 BASE = (0, 6, 18, 36)
 SLOT0 = (0, 2, 6, 12)
-STRIDE_PEER = 37
-STRIDE_CHIP = 27
-DELAY = True
+SKEW_Y = 2
+SKEW_Z = 3
+EARLY = 14
 
 
 def dot_nt(a, b):
@@ -46,32 +46,37 @@
     return sec, bulk, sec * 32 + bulk
 
 
-def peer_of(step, sec, bulk):
-    d = lax.rem(step * STRIDE_PEER, N_DEV)
-    ty = lax.rem(sec + d // 32, 4)
-    tx = lax.rem(bulk // 8 + lax.rem(d // 8, 4), 4)
-    tz = lax.rem(lax.rem(bulk // 2, 4) + lax.rem(d // 2, 4), 4)
-    tc = lax.rem(lax.rem(bulk, 2) + lax.rem(d, 2), 2)
-    tb = (tx * 4 + tz) * 2 + tc
-    return ty, tb, ty * 32 + tb
-
-
-def chip_peer(step, core, sec, bulk):
-    d = lax.rem(step * STRIDE_CHIP, N_DEV // 2)
-    ty = lax.rem(sec + d // 16, 4)
-    tx = lax.rem(bulk // 8 + lax.rem(d // 4, 4), 4)
-    tz = lax.rem(lax.rem(bulk // 2, 4) + lax.rem(d, 4), 4)
-    tb = (tx * 4 + tz) * 2 + core
-    return ty, tb, ty * 32 + tb
+def wrap(x):
+    return x - jnp.where(x >= 4, 4, 0)
+
+
+def each_peer(sec, bulk, act, core=None):
+    bx, bz, bc = bulk // 8, lax.rem(bulk // 2, 4), lax.rem(bulk, 2)
+    columns = [wrap(bx + dx) * 8 for dx in range(4)]
+    cores = [bc, 1 - bc] if core is None else [core]
+
+    def block(step, first):
+        ty0, tz0 = wrap(sec + step // 4), wrap(bz + lax.rem(step, 4))
+        for m in range(first, 4 * len(cores)):
+            dx = m % 4
+            ty = wrap(ty0 + (SKEW_Y * dx) % 4)
+            tb = columns[dx] + wrap(tz0 + (SKEW_Z * dx) % 4) * 2 + cores[m // 4]
+            act(step, ty, tb, ty * 32 + tb)
+
+    block(jnp.int32(0), 1)
+
+    def body(step, carry):
+        block(step, 0)
+        return carry
+
+    lax.fori_loop(1, 16, body, 0)
 
 
 def greet_all(barrier, sec, bulk):
-    def greet(step, carry):
-        ty, tb, _ = peer_of(step, sec, bulk)
+    def greet(step, ty, tb, t):
         pl.semaphore_signal(barrier, inc=1, device_id=(ty, tb), device_id_type=MESH)
-        return carry
-
-    lax.fori_loop(1, N_DEV, greet, 0)
+
+    each_peer(sec, bulk, greet)
 
 
 def split3(nodal, scratch):
@@ -127,7 +132,28 @@
     spread[...] = jnp.where(iota((LEVEL, LEVEL), 0) == source, 1.0, 0.0).astype(BF16)
 
 
-def prepare_send(strain, pmap, state, stage, send, spread, flat, srows, load):
+def to_rows(rows):
+    n = iota((1, 8 * rows), 1)
+    target = lax.rem(n, rows) * 8 + n // rows
+    return jnp.where(iota((8 * rows, 8 * rows), 0) == target, 1.0, 0.0).astype(BF16)
+
+
+def to_slots(rows):
+    n = iota((1, 8 * rows), 1)
+    target = lax.rem(n, 8) * rows + n // 8
+    return jnp.where(iota((8 * rows, 8 * rows), 0) == target, 1.0, 0.0).astype(BF16)
+
+
+def two_rows(first, second):
+    return jnp.concatenate([first, second], axis=0).astype(BF16)
+
+
+def side_by_side(ref, at, rows):
+    parts = [ref[pl.ds(at + 8 * i, 8)].reshape(8 * rows, 128) for i in range(2)]
+    return jnp.concatenate(parts, axis=1)
+
+
+def prepare_send(strain, pmap, state, ends, mixed, slots, send, spread, flat, srows, load):
     srows[...] = jnp.zeros_like(srows)
     for i in range(6):
         srows[i : i + 1, :] = strain[i]
@@ -159,27 +185,39 @@
             mine = dot_nn(pick, state[:, a * LEVEL : (a + 1) * LEVEL])
             flat[at * 128 : (at + 1) * 128, :] = mine.astype(BF16)
             at += 1
-        stage[pl.ds(60 + k, N_DEV, stride=MSG), :] = dot_nt(pick, strain_low)
+        ends[k] = dot_nt(pick, strain_low)
     for jj in range(3):
         for half in range(2):
             got = dot_nn(
                 flat[half * 640 : (half + 1) * 640, :], spread[:, jj * 256 : (jj + 1) * 256]
             )
             for i in range(5):
-                at = half * 5 + i
-                for j in range(2):
-                    stage[pl.ds(at * 6 + jj * 2 + j, N_DEV, stride=MSG), :] = got[
-                        i * 128 : (i + 1) * 128, j * 128 : (j + 1) * 128
-                    ]
-
-    def lower(i, carry):
-        at = pl.multiple_of(i * 2 * MSG, 2 * MSG)
-        send[pl.ds(i * 2, 2)] = (
-            stage[pl.ds(at, 2 * MSG), :].astype(BF16).reshape(2, MSG, 128)
-        )
+                row = (half * 5 + i) * 6 + jj * 2
+                for ob in range(16):
+                    part = got[i * 128 + ob * 8 : i * 128 + ob * 8 + 8]
+                    lane = (ob % 2) * 128
+                    mixed[ob // 2, row * 8 : row * 8 + 16, lane : lane + 128] = two_rows(
+                        part[:, :128], part[:, 128:]
+                    )
+    for k in (0, 2):
+        for ob in range(16):
+            lane = (ob % 2) * 128
+            at = (60 + k) * 8
+            mixed[ob // 2, at : at + 16, lane : lane + 128] = two_rows(
+                ends[k, ob * 8 : ob * 8 + 8], ends[k + 1, ob * 8 : ob * 8 + 8]
+            )
+    slots[...] = to_slots(MSG)
+
+    def lower(g, carry):
+        for m in range(2):
+            got = dot_nn(slots[m * 256 : (m + 1) * 256, :], mixed[g]).astype(BF16)
+            for i in range(2):
+                send[pl.ds(16 * g + 8 * i + 4 * m, 4)] = got[
+                    :, i * 128 : (i + 1) * 128
+                ].reshape(4, MSG, 128)
         return carry
 
-    lax.fori_loop(0, N_DEV // 2, lower, 0, unroll=4)
+    lax.fori_loop(0, 8, lower, 0)
 
 
 def make_tables(vols, off_row, off_col, vcls, chrow, ridx, inv, last, prev, crow, ccol, cvol):
@@ -247,10 +285,10 @@
     disp, load_ref, conn, grads, volume_ref, pmap, vols, affine, diag_n, off_n, off_row,
     off_col, off_count, coupling_hbm, diag_hbm, off_hbm, state_hbm,
     tail, body, residual_ref, product_ref, update_ref,
-    fluct, stage, send, spread, flat, srows, small, small_e,
+    fluct, ends, mixed, slots, rows_of, turned, send, spread, flat, srows, small, small_e,
     got, back, coupling, diag, off,
     state, low, chain, mask, strain, rdiag, cscale, dinv, weights, aff,
-    tails, wide, mine, norms,
+    tails, parts, mine, norms,
     vcls, chrow, ridx, inv, last, prev, crow, ccol, cvol,
     load_sems, own_sems, go_send, go_recv, tail_send, tail_recv, body_send, body_recv,
     norm_send, norm_recv,
@@ -266,31 +304,25 @@
         loads[-1].start()
     greet_all(barrier, sec, bulk)
     macro = strain_rows(gather_nodes(disp[...], conn, small), grads)
-    prepare_send(macro, pmap, fluct, stage, send, spread, flat, srows, loads[0])
+    prepare_send(macro, pmap, fluct, ends, mixed, slots, send, spread, flat, srows, loads[0])
     own = pltpu.make_async_copy(send.at[me], got.at[core, me // 2], own_sems.at[0])
     own.start()
     pl.semaphore_wait(barrier, N_DEV - 1)
 
-    def push(step, carry):
-        ty, tb, t = peer_of(step, sec, bulk)
+    def push(step, ty, tb, t):
+        late = jnp.where(step >= EARLY, 1, 0)
         pltpu.make_async_remote_copy(
             src_ref=send.at[t],
             dst_ref=got.at[core, me // 2],
             send_sem=go_send,
-            recv_sem=go_recv.at[core],
+            recv_sem=go_recv.at[core, late],
             device_id=(ty, tb),
             device_id_type=MESH,
         ).start()
-        return carry
-
-    if DELAY:
-
-        @pl.when(core == 0)
-        def _():
-            lax.fori_loop(1, N_DEV, push, 0)
-
-    else:
-        lax.fori_loop(1, N_DEV, push, 0)
+
+    @pl.when(core == 0)
+    def _():
+        each_peer(sec, bulk, push)
 
     make_tables(vols, off_row, off_col, vcls, chrow, ridx, inv, last, prev, crow, ccol, cvol)
     lanes6 = iota((36, 128), 1)
@@ -317,60 +349,69 @@
         return carry
 
     lax.fori_loop(0, ROWS, prepare, 0, unroll=2)
+    rows_of[...] = to_rows(MSG)
     chain[0] = jnp.zeros((192, 128), F32)
     live = off_count[0]
     own.wait()
 
     def phase(p, carry):
+        early = 4 * EARLY
+
         @pl.when(core == p)
         def _():
-            part = got.at[p, pl.ds(0, 63)]
-            pltpu.make_async_copy(part, part, go_recv.at[p]).wait()
+            part = got.at[p, pl.ds(0, early - 1)]
+            pltpu.make_async_copy(part, part, go_recv.at[p, 0]).wait()
 
         @pl.when(core != p)
         def _():
-            part = got.at[p]
-            pltpu.make_async_copy(part, part, go_recv.at[p]).wait()
-
-        if DELAY:
-
-            @pl.when((p == 0) & (core == 1))
-            def _():
-                lax.fori_loop(1, N_DEV, push, 0)
-
-        def widen(i, c2):
-            at = pl.multiple_of(i * 2 * MSG, 2 * MSG)
-            stage[pl.ds(at, 2 * MSG), :] = (
-                got[p, pl.ds(2 * i, 2)].astype(F32).reshape(2 * MSG, 128)
-            )
-            return c2
-
-        lax.fori_loop(0, 32, widen, 0, unroll=4)
-        rest = [stage[pl.ds(60 + k, 64, stride=MSG), :] for k in range(4)]
-        for c in range(4):
-            for h in range(2):
+            part = got.at[p, pl.ds(0, early)]
+            pltpu.make_async_copy(part, part, go_recv.at[p, 0]).wait()
+
+        @pl.when((p == 0) & (core == 1))
+        def _():
+            each_peer(sec, bulk, push)
+
+        part = got.at[p, pl.ds(0, 64 - early)]
+        pltpu.make_async_copy(part, part, go_recv.at[p, 1]).wait()
+
+        def take(g, c2):
+            h = g // 2
+            q0 = pl.multiple_of(lax.rem(g, 2) * 16, 16)
+            turned[...] = dot_nn(rows_of[...], side_by_side(got.at[p], 16 * g, MSG))
+
+            def message_row(r):
+                part = turned[r * 8 : r * 8 + 8, :]
+                return jnp.concatenate([part[:, :128], part[:, 128:]], axis=0)
+
+            rest = [message_row(60 + k) for k in range(4)]
+            for c in range(4):
                 v = vcls[c * 2 + h].astype(F32)
-                picked = jnp.zeros((32, 128), F32)
+                picked = jnp.zeros((16, 128), F32)
                 for k in range(4):
-                    part = rest[k][h * 32 : (h + 1) * 32]
-                    m = jnp.where(jnp.broadcast_to(part[:, 8:9], (32, 128)) == v, 1.0, 0.0)
-                    mask[(c * 2 + h) * 4 + k] = m
-                    picked = picked + m * part
+                    code = jnp.broadcast_to(rest[k][:, 8:9], (16, 128))
+                    m = jnp.where(code == v, 1.0, 0.0)
+                    mask[c * 4 + k] = m
+                    picked = picked + m * rest[k]
                 for i in range(6):
-                    strain[(c * 2 + h) * 6 + i] = jnp.broadcast_to(picked[:, i : i + 1], (32, 128))
-        for h in range(2):
+                    strain[(c * 2 + h) * 6 + i, pl.ds(q0, 16), :] = jnp.broadcast_to(
+                        picked[:, i : i + 1], (16, 128)
+                    )
             for a in range(4):
                 for j in range(6):
                     sums = {}
                     for k in range(a, 4):
-                        part = stage[pl.ds(h * 32 * MSG + BASE[k] + a * 6 + j, 32, stride=MSG), :]
+                        part = message_row(BASE[k] + a * 6 + j)
                         for c in range(a, 4):
-                            term = mask[(c * 2 + h) * 4 + k] * part
+                            term = mask[c * 4 + k] * part
                             sums[c] = sums[c] + term if c in sums else term
                     for c in range(a, 4):
                         i = static_row(c, h, a)
-                        state[i, j * 32 : (j + 1) * 32, :] = sums[c]
-                        low[i, j * 32 : (j + 1) * 32, :] = sums[c].astype(BF16)
+                        at = pl.multiple_of(j * 32 + q0, 16)
+                        state[i, pl.ds(at, 16), :] = sums[c]
+                        low[i, pl.ds(at, 16), :] = sums[c].astype(BF16)
+            return c2
+
+        lax.fori_loop(0, 4, take, 0)
 
         def row_scale(i, c2):
             r = ridx[i]
@@ -401,7 +442,7 @@
                 chain[c + 1] = chain[prev[c]] + scaled
                 return c3
 
-            lax.fori_loop(0, OFF, contact, 0, unroll=4)
+            lax.fori_loop(0, OFF, contact, 0, unroll=16)
 
             def update(i, c3):
                 r = ridx[i]
@@ -413,14 +454,15 @@
                 low[i] = new.astype(BF16)
                 return c3
 
-            lax.fori_loop(0, ROWS, update, 0, unroll=4)
+            lax.fori_loop(0, ROWS, update, 0, unroll=10)
             return c2
 
         lax.fori_loop(0, SWEEPS, sweep, 0)
 
         lane = iota((32, 128), 1)
-        for c in range(4):
-            for h in range(2):
+        for h in range(2):
+            last_rows = []
+            for c in range(4):
                 acc = jnp.zeros((192, 128), F32)
                 for a in range(c + 1):
                     i = static_row(c, h, a)
@@ -428,30 +470,43 @@
                     high = low[i]
                     acc = acc + dot_nt(high, weights[i])
                     acc = acc + dot_nt((x - high.astype(F32)).astype(BF16), weights[i])
-                    for j in range(6):
-                        stage[pl.ds(h * 32 * MSG + BASE[c] + a * 6 + j, 32, stride=MSG), :] = x[
-                            j * 32 : (j + 1) * 32
-                        ]
+                    for j in range(0, 6, 2):
+                        at = (BASE[c] + a * 6 + j) * 8
+                        for q in range(4):
+                            cols = (q % 2) * 128
+                            mixed[h * 2 + q // 2, at : at + 16, cols : cols + 128] = two_rows(
+                                x[j * 32 + q * 8 : j * 32 + q * 8 + 8],
+                                x[j * 32 + 32 + q * 8 : j * 32 + 40 + q * 8],
+                            )
                 t = acc[0:32]
                 for j in range(1, 6):
                     t = t + pltpu.roll(acc[j * 32 : (j + 1) * 32], 8 * j, axis=1)
                 t = t + pltpu.roll(t, 64, axis=1)
                 v = vcls[c * 2 + h]
                 tangent = aff[v] - t / (128.0 * (c + 1))
-                row = jnp.where(lane < 48, tangent, jnp.where(lane == 64, v.astype(F32), 0.0))
-                stage[pl.ds(h * 32 * MSG + 60 + c, 32, stride=MSG), :] = row
-
-        def lower(i, c2):
-            at = pl.multiple_of(i * 2 * MSG, 2 * MSG)
-            back[p, pl.ds(2 * i, 2)] = (
-                stage[pl.ds(at, 2 * MSG), :].astype(BF16).reshape(2, MSG, 128)
-            )
+                last_rows.append(
+                    jnp.where(lane < 48, tangent, jnp.where(lane == 64, v.astype(F32), 0.0))
+                )
+            for k in (0, 2):
+                at = (60 + k) * 8
+                for q in range(4):
+                    cols = (q % 2) * 128
+                    mixed[h * 2 + q // 2, at : at + 16, cols : cols + 128] = two_rows(
+                        last_rows[k][q * 8 : q * 8 + 8], last_rows[k + 1][q * 8 : q * 8 + 8]
+                    )
+
+        def lower(g, c2):
+            for m in range(2):
+                out = dot_nn(slots[m * 256 : (m + 1) * 256, :], mixed[g]).astype(BF16)
+                for i in range(2):
+                    back[p, pl.ds(16 * g + 8 * i + 4 * m, 4)] = out[
+                        :, i * 128 : (i + 1) * 128
+                    ].reshape(4, MSG, 128)
             return c2
 
-        lax.fori_loop(0, 32, lower, 0, unroll=4)
-
-        def push_tail(step, c2):
-            ty, tb, t = chip_peer(step, p, sec, bulk)
+        lax.fori_loop(0, 4, lower, 0)
+
+        def push_tail(step, ty, tb, t):
             pltpu.make_async_remote_copy(
                 src_ref=back.at[p, t // 2, pl.ds(48, 16)],
                 dst_ref=tails.at[me],
@@ -460,10 +515,8 @@
                 device_id=(ty, tb),
                 device_id_type=MESH,
             ).start()
-            return c2
-
-        def push_body(step, c2):
-            ty, tb, t = chip_peer(step, p, sec, bulk)
+
+        def push_body(step, ty, tb, t):
             pltpu.make_async_remote_copy(
                 src_ref=back.at[p, t // 2, pl.ds(0, 48)],
                 dst_ref=body.at[me],
@@ -472,19 +525,14 @@
                 device_id=(ty, tb),
                 device_id_type=MESH,
             ).start()
-            return c2
-
-        lax.fori_loop(1, N_DEV // 2, push_tail, 0)
-
-        @pl.when(core != p)
-        def _():
-            push_tail(0, 0)
-
-        lax.fori_loop(1, N_DEV // 2, push_body, 0)
-
-        @pl.when(core != p)
-        def _():
-            push_body(0, 0)
+
+        partner = bulk + 1 - 2 * core
+        for push_part in (push_tail, push_body):
+            each_peer(sec, bulk, push_part, p)
+
+            @pl.when(core != p)
+            def _():
+                push_part(0, sec, partner, sec * 32 + partner)
 
         return carry
 
@@ -502,12 +550,19 @@
     own_tail.wait()
     landed = tails.at[pl.ds(0, N_DEV - 1)]
     pltpu.make_async_copy(landed, landed, tail_recv).wait()
-    wide[...] = tails[...].astype(F32).reshape(N_DEV * 16, 128)
     keep = pltpu.make_async_copy(tails, tail, own_sems.at[2])
     keep.start()
+    turn = to_rows(16)[96:128]
+    for g in range(8):
+        out = dot_nn(turn, side_by_side(tails, 16 * g, 16))
+        for c in range(4):
+            for i in range(2):
+                parts[c, 16 * g + 8 * i : 16 * g + 8 * i + 8, :] = out[
+                    c * 8 : c * 8 + 8, i * 128 : (i + 1) * 128
+                ]
     tangent = jnp.zeros((128, ELEM), F32)
     for c in range(4):
-        part = wide[pl.ds(12 + c, N_DEV, stride=16), :]
+        part = parts[c]
         code = jnp.broadcast_to(part[:, 64:65], (N_DEV, ELEM))
         pick = jnp.where(same_owner & (code == volume), 1.0, 0.0).astype(BF16)
         tangent = tangent + dot_nn(jnp.transpose(part).astype(BF16), pick)
@@ -523,8 +578,7 @@
     )
     norms[me] = mine[...]
 
-    def push_norm(step, carry):
-        ty, tb, t = peer_of(step, sec, bulk)
+    def push_norm(step, ty, tb, t):
         pltpu.make_async_remote_copy(
             src_ref=mine,
             dst_ref=norms.at[me],
@@ -533,9 +587,8 @@
             device_id=(ty, tb),
             device_id_type=MESH,
         ).start()
-        return carry
-
-    lax.fori_loop(1, N_DEV, push_norm, 0)
+
+    each_peer(sec, bulk, push_norm)
     trial = strain_rows(gather_nodes(residual, conn, small), grads)
     product_ref[...] = assemble(grads, conn, apply_tangent(tangent, trial, weight), small_e)
     arrived = norms.at[pl.ds(0, N_DEV - 1)]
@@ -558,20 +611,30 @@
 def unpack_kernel(
     residual, product, update, tail, body, pmap,
     out_residual, out_product, out_update, out_hbm,
-    stage, spread, rows, flat, result, sems,
+    parts, spread, rows, flat, result, sems,
 ):
     out_residual[...] = residual[...]
     out_product[...] = product[...]
     out_update[...] = update[...]
     make_spread(spread)
 
-    def widen(i, carry):
-        at = pl.multiple_of(i * MSG, MSG)
-        stage[pl.ds(at, 48), :] = body[i].astype(F32)
-        stage[pl.ds(at + 48, 16), :] = tail[i].astype(F32)
-        return carry
-
-    lax.fori_loop(0, N_DEV, widen, 0, unroll=8)
+    turn_body = to_rows(48)
+    turn_tail = to_rows(16)
+    for g in range(8):
+        main = dot_nn(turn_body, side_by_side(body, 16 * g, 48))
+        end = dot_nn(turn_tail, side_by_side(tail, 16 * g, 16))
+        for r in range(60):
+            source, at = (main, r) if r < 48 else (end, r - 48)
+            part = source[at * 8 : at * 8 + 8]
+            rows[r // 6, 16 * g : 16 * g + 16, (r % 6) * 128 : (r % 6 + 1) * 128] = two_rows(
+                part[:, :128], part[:, 128:]
+            )
+        for c in range(4):
+            part = end[(12 + c) * 8 : (12 + c) * 8 + 8]
+            for i in range(2):
+                parts[c, 16 * g + 8 * i : 16 * g + 8 * i + 8, :] = part[
+                    :, i * 128 : (i + 1) * 128
+                ]
     where_to = pmap[...].astype(F32)
     column = jnp.transpose(jnp.broadcast_to(where_to, (128, ELEM))).astype(I32)
     owner = column // ELEM
@@ -579,18 +642,14 @@
     same_owner = iota((ELEM, N_DEV), 1) == owner
     picks = []
     for c in range(4):
-        part = stage[pl.ds(60 + c, N_DEV, stride=MSG), :]
-        code = jnp.transpose(part)[64:65, :].astype(I32)
+        code = jnp.transpose(parts[c])[64:65, :].astype(I32)
         picks.append(jnp.where(same_owner & (code == volume), 1.0, 0.0).astype(BF16))
     pick = jnp.concatenate(picks, axis=1)
     copies = []
     for a in range(4):
         for c in range(a, 4):
-            for j in range(6):
-                rows[c * 128 : (c + 1) * 128, j * 128 : (j + 1) * 128] = stage[
-                    pl.ds(BASE[c] + a * 6 + j, N_DEV, stride=MSG), :
-                ].astype(BF16)
-        flat[a * 128 :, :] = dot_nt(rows[a * 128 :, :], spread[...]).astype(BF16)
+            level = rows[BASE[c] // 6 + a]
+            flat[c * 128 : (c + 1) * 128, :] = dot_nt(level, spread[...]).astype(BF16)
         result[:, a * LEVEL : (a + 1) * LEVEL] = dot_nn(
             pick[:, a * 128 :], flat[a * 128 :, :]
         ).astype(BF16)
@@ -678,7 +737,11 @@
         out_specs=(ANY, ANY, VMEM, VMEM, VMEM),
         scratch_shapes=[
             vmem((ELEM, 4 * LEVEL), BF16),
-            vmem((N_DEV * MSG, 128), F32),
+            vmem((4, N_DEV, 128), F32),
+            vmem((8, 512, 256), BF16),
+            vmem((512, 512), BF16),
+            vmem((512, 512), BF16),
+            vmem((512, 256), F32),
             vmem((N_DEV, MSG, 128), BF16),
             vmem((LEVEL, LEVEL), BF16),
             vmem((1280, LEVEL), BF16),
@@ -693,7 +756,7 @@
             vmem((ROWS, 192, 128), F32),
             vmem((ROWS, 192, 128), BF16),
             vmem((OFF + 1, 192, 128), F32),
-            vmem((32, 32, 128), F32),
+            vmem((16, 16, 128), F32),
             vmem((48, 32, 128), F32),
             vmem((ROWS, 32, 128), F32),
             vmem((OFF, 32, 128), F32),
@@ -701,12 +764,12 @@
             vmem((ROWS, 128, 128), BF16),
             vmem((8, 1, 128), F32),
             vmem((N_DEV, 16, 128), BF16),
-            vmem((N_DEV * 16, 128), F32),
+            vmem((4, N_DEV, 128), F32),
             vmem((8, 128), F32),
             vmem((N_DEV, 8, 128), F32),
             smem(8), smem(ROWS), smem(ROWS), smem(ROWS), smem(ROWS),
             smem(OFF), smem(OFF), smem(OFF), smem(OFF),
-            DMA((4,)), DMA((3,)), DMA, DMA((2,)), DMA, DMA, DMA, DMA, DMA, DMA,
+            DMA((4,)), DMA((3,)), DMA, DMA((2, 2)), DMA, DMA, DMA, DMA, DMA, DMA,
         ],
         compiler_params=params(1, 60),
         name="step",
@@ -722,9 +785,9 @@
         in_specs=[VMEM] * 6,
         out_specs=(VMEM, VMEM, VMEM, ANY),
         scratch_shapes=[
-            vmem((N_DEV * MSG, 128), F32),
+            vmem((4, N_DEV, 128), F32),
             vmem((LEVEL, LEVEL), BF16),
-            vmem((512, LEVEL), BF16),
+            vmem((10, N_DEV, LEVEL), BF16),
             vmem((512, LEVEL), BF16),
             vmem((ELEM, 4 * LEVEL), BF16),
             DMA((4,)),

time: 104 us -> 89.6 us (0.86)
  Pallas kernels: 103 us -> 87.9 us
    pallas_call x1, Pallas kernels: 93.7 us -> 78.7 us  [on_device(): pl.pallas_call(step_kernel, out_shape=(jax.ShapeDtypeStruct((N_DEV, 16, 1...]
where the time goes in v3:
time: 89.6 us; the launch traced here: 89.3 us
  Pallas kernels  87.9 us (98%)
  between operations  1.45 us (2%)
    pallas_call x1, Pallas kernels, on_device(): pl.pallas_call(step_kernel, out_shape=(jax.ShapeDtypeStruct((N_DEV, 16, 1...  78.7 us
    pallas_call x1, Pallas kernels, on_device(): pl.pallas_call(unpack_kernel, out_shape=(nodal, nodal, nodal, jax.ShapeDt...  9.2 us

profile of v3, /device:TPU:1, one launch (start us, length us, event | category | flops | bytes accessed | tf_op | source)
XLA Modules:
  0.0 89.3 jit_solution(5108615905925551618)
XLA Ops:
  1.3 78.7 %step.1 = (bf16[128,16,128]{2,1,0:T(8,128)(2,1)}, bf16[128,48,128]{2,1,0:T(8,128)(2,1)}, f32[3,128]{1,0:T(4,128)}, f32[3,128]{1,0:T(4,128)}, f32[3,128]{1,0:T(4,128)}) custom-call(f32[3,128]{1,0:T(4,128)} %disp.1, f32[3,128]{1,0:T(4,128)} %load_ref.1, s32[4,512]{1,0:T(4,128)} %conn.1, f32[12,512]{1,0:T(8,128)} %grads.1, f32[1,512]{1,0:T(1,128)} %bitcast.16, ...), custom_call_target="tpu_custom_call" | custom-call | tf_op jit(solution)/shard_map/step/pallas_call | solution.py:729
  80.0 9.2 %unpack.1 = (f32[3,128]{1,0:T(4,128)}, f32[3,128]{1,0:T(4,128)}, f32[3,128]{1,0:T(4,128)}, bf16[512,3072]{1,0:T(8,128)(2,1)}) custom-call(f32[3,128]{1,0:T(4,128)} %get-tuple-element.9.residual, f32[3,128]{1,0:T(4,128)} %get-tuple-element.10.product, f32[3,128]{1,0:T(4,128)} %get-tuple-element.11.update, bf16[128,16,128]{2,1,0:T(8,128)(2,1)} %get-tuple-element.12.tail, ...), custom_call_target="tpu_custom_call" | custom-call | tf_op jit(solution)/shard_map/unpack/pallas_call | solution.py:782

commit v4 on v3

--- a/solution.py
+++ b/solution.py
@@ -19,9 +19,11 @@
 MESH = pl.DeviceIdType.MESH
 BASE = (0, 6, 18, 36)
 SLOT0 = (0, 2, 6, 12)
+LEVEL0 = (0, 4, 7, 9)
 SKEW_Y = 2
 SKEW_Z = 3
 EARLY = 14
+SPLIT = 8
 
 
 def dot_nt(a, b):
@@ -50,7 +52,7 @@
     return x - jnp.where(x >= 4, 4, 0)
 
 
-def each_peer(sec, bulk, act, core=None):
+def each_peer(sec, bulk, act, core=None, begin=0, end=16):
     bx, bz, bc = bulk // 8, lax.rem(bulk // 2, 4), lax.rem(bulk, 2)
     columns = [wrap(bx + dx) * 8 for dx in range(4)]
     cores = [bc, 1 - bc] if core is None else [core]
@@ -63,13 +65,14 @@
             tb = columns[dx] + wrap(tz0 + (SKEW_Z * dx) % 4) * 2 + cores[m // 4]
             act(step, ty, tb, ty * 32 + tb)
 
-    block(jnp.int32(0), 1)
+    if begin == 0:
+        block(jnp.int32(0), 1)
 
     def body(step, carry):
         block(step, 0)
         return carry
 
-    lax.fori_loop(1, 16, body, 0)
+    lax.fori_loop(max(begin, 1), end, body, 0)
 
 
 def greet_all(barrier, sec, bulk):
@@ -148,9 +151,25 @@
     return jnp.concatenate([first, second], axis=0).astype(BF16)
 
 
-def side_by_side(ref, at, rows):
-    parts = [ref[pl.ds(at + 8 * i, 8)].reshape(8 * rows, 128) for i in range(2)]
+def side_by_side(ref, at, tile):
+    parts = [
+        ref[pl.ds(at + 8 * i, 8), tile * 16 : tile * 16 + 16, :].reshape(128, 128)
+        for i in range(2)
+    ]
     return jnp.concatenate(parts, axis=1)
+
+
+def write_messages(slots, mixed, target, count):
+    def lower(g, carry):
+        for tile in range(4):
+            out = dot_nn(slots, mixed[g, tile * 128 : tile * 128 + 128, :]).astype(BF16)
+            for i in range(2):
+                target[pl.ds(16 * g + 8 * i, 8), tile * 16 : tile * 16 + 16, :] = out[
+                    :, i * 128 : (i + 1) * 128
+                ].reshape(8, 16, 128)
+        return carry
+
+    lax.fori_loop(0, count, lower, 0, unroll=2)
 
 
 def prepare_send(strain, pmap, state, ends, mixed, slots, send, spread, flat, srows, load):
@@ -165,11 +184,12 @@
     make_spread(spread)
     load.wait()
 
-    ones = jnp.ones((16, LEVEL), BF16)
-    levels = jnp.zeros((1, ELEM), I32)
+    ones = jnp.ones((LEVEL, 128), BF16)
+    levels = jnp.zeros((ELEM, 128), F32)
     for a in range(4):
-        weight = dot_nt(ones, jnp.abs(state[:, a * LEVEL : (a + 1) * LEVEL]))[0:1, :]
-        levels = jnp.where(weight > 0.0, a + 1, levels)
+        weight = dot_nn(jnp.abs(state[:, a * LEVEL : (a + 1) * LEVEL]), ones)
+        levels = jnp.where(weight > 0.0, a + 1.0, levels)
+    levels = jnp.transpose(levels)[0:1, :].astype(I32)
     key = (owner * 4096 + levels * 512 + iota((1, ELEM), 1)).astype(F32)
     key_col = jnp.transpose(jnp.broadcast_to(key, (128, ELEM)))
     order = []
@@ -178,21 +198,26 @@
         order.append(jnp.sum(jnp.where(key_col < part, 1.0, 0.0), axis=0, keepdims=True))
     order = jnp.concatenate(order, axis=1).astype(I32)
 
-    at = 0
+    picks = []
     for k in range(4):
         pick = jnp.where(order == iota((N_DEV, ELEM), 0) * 4 + k, 1.0, 0.0).astype(BF16)
-        for a in range(k + 1):
-            mine = dot_nn(pick, state[:, a * LEVEL : (a + 1) * LEVEL])
-            flat[at * 128 : (at + 1) * 128, :] = mine.astype(BF16)
-            at += 1
         ends[k] = dot_nt(pick, strain_low)
+        picks.append(pick)
+    picks = jnp.concatenate(picks, axis=0)
+    for a in range(4):
+        at, end = LEVEL0[a] * 128, (LEVEL0[a] + 4 - a) * 128
+        flat[at:end, :] = dot_nn(
+            picks[a * 128 :], state[:, a * LEVEL : (a + 1) * LEVEL]
+        ).astype(BF16)
+    places = [(k, a) for a in range(4) for k in range(a, 4)]
     for jj in range(3):
         for half in range(2):
             got = dot_nn(
                 flat[half * 640 : (half + 1) * 640, :], spread[:, jj * 256 : (jj + 1) * 256]
             )
             for i in range(5):
-                row = (half * 5 + i) * 6 + jj * 2
+                k, a = places[half * 5 + i]
+                row = BASE[k] + a * 6 + jj * 2
                 for ob in range(16):
                     part = got[i * 128 + ob * 8 : i * 128 + ob * 8 + 8]
                     lane = (ob % 2) * 128
@@ -206,18 +231,8 @@
             mixed[ob // 2, at : at + 16, lane : lane + 128] = two_rows(
                 ends[k, ob * 8 : ob * 8 + 8], ends[k + 1, ob * 8 : ob * 8 + 8]
             )
-    slots[...] = to_slots(MSG)
-
-    def lower(g, carry):
-        for m in range(2):
-            got = dot_nn(slots[m * 256 : (m + 1) * 256, :], mixed[g]).astype(BF16)
-            for i in range(2):
-                send[pl.ds(16 * g + 8 * i + 4 * m, 4)] = got[
-                    :, i * 128 : (i + 1) * 128
-                ].reshape(4, MSG, 128)
-        return carry
-
-    lax.fori_loop(0, 8, lower, 0)
+    slots[...] = to_slots(16)
+    write_messages(slots[...], mixed, send, 8)
 
 
 def make_tables(vols, off_row, off_col, vcls, chrow, ridx, inv, last, prev, crow, ccol, cvol):
@@ -349,10 +364,30 @@
         return carry
 
     lax.fori_loop(0, ROWS, prepare, 0, unroll=2)
-    rows_of[...] = to_rows(MSG)
+    rows_of[...] = to_rows(16)
     chain[0] = jnp.zeros((192, 128), F32)
     live = off_count[0]
     own.wait()
+
+    partner = bulk + 1 - 2 * core
+
+    def send_back(p, first, rows, target, send_sem, recv_sem, begin=0, end=16):
+        def push_back(step, ty, tb, t):
+            pltpu.make_async_remote_copy(
+                src_ref=back.at[p, t // 2, pl.ds(first, rows)],
+                dst_ref=target.at[me],
+                send_sem=send_sem,
+                recv_sem=recv_sem,
+                device_id=(ty, tb),
+                device_id_type=MESH,
+            ).start()
+
+        each_peer(sec, bulk, push_back, p, begin, end)
+        if begin == 0:
+
+            @pl.when(core != p)
+            def _():
+                push_back(0, sec, partner, sec * 32 + partner)
 
     def phase(p, carry):
         early = 4 * EARLY
@@ -377,7 +412,10 @@
         def take(g, c2):
             h = g // 2
             q0 = pl.multiple_of(lax.rem(g, 2) * 16, 16)
-            turned[...] = dot_nn(rows_of[...], side_by_side(got.at[p], 16 * g, MSG))
+            for tile in range(4):
+                turned[tile * 128 : tile * 128 + 128, :] = dot_nn(
+                    rows_of[...], side_by_side(got.at[p], 16 * g, tile)
+                )
 
             def message_row(r):
                 part = turned[r * 8 : r * 8 + 8, :]
@@ -495,48 +533,18 @@
                         last_rows[k][q * 8 : q * 8 + 8], last_rows[k + 1][q * 8 : q * 8 + 8]
                     )
 
-        def lower(g, c2):
-            for m in range(2):
-                out = dot_nn(slots[m * 256 : (m + 1) * 256, :], mixed[g]).astype(BF16)
-                for i in range(2):
-                    back[p, pl.ds(16 * g + 8 * i + 4 * m, 4)] = out[
-                        :, i * 128 : (i + 1) * 128
-                    ].reshape(4, MSG, 128)
-            return c2
-
-        lax.fori_loop(0, 4, lower, 0)
-
-        def push_tail(step, ty, tb, t):
-            pltpu.make_async_remote_copy(
-                src_ref=back.at[p, t // 2, pl.ds(48, 16)],
-                dst_ref=tails.at[me],
-                send_sem=tail_send,
-                recv_sem=tail_recv,
-                device_id=(ty, tb),
-                device_id_type=MESH,
-            ).start()
-
-        def push_body(step, ty, tb, t):
-            pltpu.make_async_remote_copy(
-                src_ref=back.at[p, t // 2, pl.ds(0, 48)],
-                dst_ref=body.at[me],
-                send_sem=body_send,
-                recv_sem=body_recv,
-                device_id=(ty, tb),
-                device_id_type=MESH,
-            ).start()
-
-        partner = bulk + 1 - 2 * core
-        for push_part in (push_tail, push_body):
-            each_peer(sec, bulk, push_part, p)
-
-            @pl.when(core != p)
-            def _():
-                push_part(0, sec, partner, sec * 32 + partner)
+        write_messages(slots[...], mixed, back.at[p], 4)
+
+        send_back(p, 48, 16, tails, tail_send, tail_recv)
+
+        @pl.when(p == 0)
+        def _():
+            send_back(0, 0, 48, body, body_send, body_recv, 0, SPLIT)
 
         return carry
 
     lax.fori_loop(0, 2, phase, 0)
+    send_back(0, 0, 48, body, body_send, body_recv, SPLIT, 16)
     mine_back = back.at[core, me // 2]
     own_tail = pltpu.make_async_copy(mine_back.at[pl.ds(48, 16)], tails.at[me], own_sems.at[0])
     own_body = pltpu.make_async_copy(mine_back.at[pl.ds(0, 48)], body.at[me], own_sems.at[1])
@@ -554,7 +562,7 @@
     keep.start()
     turn = to_rows(16)[96:128]
     for g in range(8):
-        out = dot_nn(turn, side_by_side(tails, 16 * g, 16))
+        out = dot_nn(turn, side_by_side(tails, 16 * g, 0))
         for c in range(4):
             for i in range(2):
                 parts[c, 16 * g + 8 * i : 16 * g + 8 * i + 8, :] = out[
@@ -574,7 +582,7 @@
     residual_ref[...] = residual
     mine[...] = jnp.broadcast_to(
         jnp.sum(jnp.sum(residual * residual, axis=1, keepdims=True), axis=0, keepdims=True),
-        (8, 128),
+        (1, 128),
     )
     norms[me] = mine[...]
 
@@ -589,11 +597,12 @@
         ).start()
 
     each_peer(sec, bulk, push_norm)
+    send_back(1, 0, 48, body, body_send, body_recv)
     trial = strain_rows(gather_nodes(residual, conn, small), grads)
     product_ref[...] = assemble(grads, conn, apply_tangent(tangent, trial, weight), small_e)
     arrived = norms.at[pl.ds(0, N_DEV - 1)]
     pltpu.make_async_copy(arrived, arrived, norm_recv).wait()
-    total = jnp.sum(norms[...], axis=0)[0:1, :]
+    total = jnp.sum(norms[...], axis=0)
     root = jnp.sqrt(total / (3.0 * 16384) + 1e-06)
     update_ref[...] = -jnp.minimum(1.0, 1.0 / root) * residual
 
@@ -609,37 +618,49 @@
 
 
 def unpack_kernel(
-    residual, product, update, tail, body, pmap,
+    residual, product, update, tail_hbm, body_hbm, pmap,
     out_residual, out_product, out_update, out_hbm,
-    parts, spread, rows, flat, result, sems,
+    tail, body, parts, spread, rows, flat, result, load_sems, sems,
 ):
+    loads = [
+        pltpu.make_async_copy(tail_hbm, tail, load_sems.at[0]),
+        pltpu.make_async_copy(body_hbm, body, load_sems.at[1]),
+    ]
+    for load in loads:
+        load.start()
     out_residual[...] = residual[...]
     out_product[...] = product[...]
     out_update[...] = update[...]
-    make_spread(spread)
-
-    turn_body = to_rows(48)
-    turn_tail = to_rows(16)
-    for g in range(8):
-        main = dot_nn(turn_body, side_by_side(body, 16 * g, 48))
-        end = dot_nn(turn_tail, side_by_side(tail, 16 * g, 16))
-        for r in range(60):
-            source, at = (main, r) if r < 48 else (end, r - 48)
-            part = source[at * 8 : at * 8 + 8]
-            rows[r // 6, 16 * g : 16 * g + 16, (r % 6) * 128 : (r % 6 + 1) * 128] = two_rows(
-                part[:, :128], part[:, 128:]
-            )
-        for c in range(4):
-            part = end[(12 + c) * 8 : (12 + c) * 8 + 8]
-            for i in range(2):
-                parts[c, 16 * g + 8 * i : 16 * g + 8 * i + 8, :] = part[
-                    :, i * 128 : (i + 1) * 128
-                ]
+    n = iota((1, LEVEL), 1)
+    source = lax.rem(n, 6) * 128 + n // 6
+    spread[...] = jnp.where(iota((LEVEL, LEVEL), 0) == source, 1.0, 0.0).astype(BF16)
+    turn = to_rows(16)
     where_to = pmap[...].astype(F32)
     column = jnp.transpose(jnp.broadcast_to(where_to, (128, ELEM))).astype(I32)
     owner = column // ELEM
     volume = lax.rem(column, ELEM) // 64
     same_owner = iota((ELEM, N_DEV), 1) == owner
+    for load in loads:
+        load.wait()
+    for tile in range(4):
+        for g in range(8):
+            source_ref, at = (body, tile) if tile < 3 else (tail, 0)
+            got = dot_nn(turn, side_by_side(source_ref, 16 * g, at))
+            for i in range(16):
+                r = tile * 16 + i
+                part = got[i * 8 : i * 8 + 8]
+                if r < 60:
+                    c = 0 if r < 6 else 1 if r < 18 else 2 if r < 36 else 3
+                    a, j = (r - BASE[c]) // 6, r % 6
+                    block = LEVEL0[a] + c - a
+                    rows[
+                        block * 128 + 16 * g : block * 128 + 16 * g + 16, j * 128 : (j + 1) * 128
+                    ] = two_rows(part[:, :128], part[:, 128:])
+                else:
+                    for side in range(2):
+                        parts[r - 60, 16 * g + 8 * side : 16 * g + 8 * side + 8, :] = part[
+                            :, side * 128 : (side + 1) * 128
+                        ]
     picks = []
     for c in range(4):
         code = jnp.transpose(parts[c])[64:65, :].astype(I32)
@@ -647,11 +668,10 @@
     pick = jnp.concatenate(picks, axis=1)
     copies = []
     for a in range(4):
-        for c in range(a, 4):
-            level = rows[BASE[c] // 6 + a]
-            flat[c * 128 : (c + 1) * 128, :] = dot_nt(level, spread[...]).astype(BF16)
+        at, end = LEVEL0[a] * 128, (LEVEL0[a] + 4 - a) * 128
+        flat[at:end, :] = dot_nn(rows[at:end, :], spread[...]).astype(BF16)
         result[:, a * LEVEL : (a + 1) * LEVEL] = dot_nn(
-            pick[:, a * 128 :], flat[a * 128 :, :]
+            pick[:, a * 128 :], flat[at:end, :]
         ).astype(BF16)
         part = pl.ds(a * LEVEL, LEVEL)
         copy = pltpu.make_async_copy(result.at[:, part], out_hbm.at[:, part], sems.at[a])
@@ -739,8 +759,8 @@
             vmem((ELEM, 4 * LEVEL), BF16),
             vmem((4, N_DEV, 128), F32),
             vmem((8, 512, 256), BF16),
-            vmem((512, 512), BF16),
-            vmem((512, 512), BF16),
+            vmem((128, 128), BF16),
+            vmem((128, 128), BF16),
             vmem((512, 256), F32),
             vmem((N_DEV, MSG, 128), BF16),
             vmem((LEVEL, LEVEL), BF16),
@@ -765,8 +785,8 @@
             vmem((8, 1, 128), F32),
             vmem((N_DEV, 16, 128), BF16),
             vmem((4, N_DEV, 128), F32),
-            vmem((8, 128), F32),
-            vmem((N_DEV, 8, 128), F32),
+            vmem((1, 128), F32),
+            vmem((N_DEV, 1, 128), F32),
             smem(8), smem(ROWS), smem(ROWS), smem(ROWS), smem(ROWS),
             smem(OFF), smem(OFF), smem(OFF), smem(OFF),
             DMA((4,)), DMA((3,)), DMA, DMA((2, 2)), DMA, DMA, DMA, DMA, DMA, DMA,
@@ -782,14 +802,17 @@
     return pl.pallas_call(
         unpack_kernel,
         out_shape=(nodal, nodal, nodal, jax.ShapeDtypeStruct((ELEM, 4 * LEVEL), BF16)),
-        in_specs=[VMEM] * 6,
+        in_specs=[VMEM, VMEM, VMEM, ANY, ANY, VMEM],
         out_specs=(VMEM, VMEM, VMEM, ANY),
         scratch_shapes=[
+            vmem((N_DEV, 16, 128), BF16),
+            vmem((N_DEV, 48, 128), BF16),
             vmem((4, N_DEV, 128), F32),
             vmem((LEVEL, LEVEL), BF16),
-            vmem((10, N_DEV, LEVEL), BF16),
-            vmem((512, LEVEL), BF16),
+            vmem((1280, LEVEL), BF16),
+            vmem((1280, LEVEL), BF16),
             vmem((ELEM, 4 * LEVEL), BF16),
+            DMA((2,)),
             DMA((4,)),
         ],
         compiler_params=params(None, 60),

time: 89.6 us -> 86.8 us (0.969)
  Pallas kernels: 87.9 us -> 85 us
    pallas_call x1, Pallas kernels: 9.2 us -> 7.42 us  [on_device(): pl.pallas_call(unpack_kernel, out_shape=(nodal, nodal, nodal, jax.ShapeDt...]
    pallas_call x1, Pallas kernels: 78.7 us -> 77.6 us  [on_device(): pl.pallas_call(step_kernel, out_shape=(jax.ShapeDtypeStruct((N_DEV, 16, 1...]
where the time goes in v4:
time: 86.8 us; the launch traced here: 86.5 us
  Pallas kernels  85 us (98%)
  between operations  1.45 us (2%)
    pallas_call x1, Pallas kernels, on_device(): pl.pallas_call(step_kernel, out_shape=(jax.ShapeDtypeStruct((N_DEV, 16, 1...  77.6 us
    pallas_call x1, Pallas kernels, on_device(): pl.pallas_call(unpack_kernel, out_shape=(nodal, nodal, nodal, jax.ShapeDt...  7.42 us

profile of v4, /device:TPU:1, one launch (start us, length us, event | category | flops | bytes accessed | tf_op | source)
XLA Modules:
  0.0 86.5 jit_solution(12527365937775423072)
XLA Ops:
  1.3 77.6 %step.1 = (bf16[128,16,128]{2,1,0:T(8,128)(2,1)}, bf16[128,48,128]{2,1,0:T(8,128)(2,1)}, f32[3,128]{1,0:T(4,128)}, f32[3,128]{1,0:T(4,128)}, f32[3,128]{1,0:T(4,128)}) custom-call(f32[3,128]{1,0:T(4,128)} %disp.1, f32[3,128]{1,0:T(4,128)} %load_ref.1, s32[4,512]{1,0:T(4,128)} %conn.1, f32[12,512]{1,0:T(8,128)} %grads.1, f32[1,512]{1,0:T(1,128)} %bitcast.16, ...), custom_call_target="tpu_custom_call" | custom-call | tf_op jit(solution)/shard_map/step/pallas_call | solution.py:749
  78.9 7.4 %unpack.1 = (f32[3,128]{1,0:T(4,128)}, f32[3,128]{1,0:T(4,128)}, f32[3,128]{1,0:T(4,128)}, bf16[512,3072]{1,0:T(8,128)(2,1)}) custom-call(f32[3,128]{1,0:T(4,128)} %get-tuple-element.9.residual, f32[3,128]{1,0:T(4,128)} %get-tuple-element.10.product, f32[3,128]{1,0:T(4,128)} %get-tuple-element.11.update, bf16[128,16,128]{2,1,0:T(8,128)(2,1)} %get-tuple-element.12.tail_hbm, ...), custom_call_target="tpu_custom_call" | custom-call | tf_op jit(solution)/shard_map/unpack/pallas_call | solution.py:802

commit v5 on v4

--- a/solution.py
+++ b/solution.py
@@ -169,7 +169,7 @@
                 ].reshape(8, 16, 128)
         return carry
 
-    lax.fori_loop(0, count, lower, 0, unroll=2)
+    lax.fori_loop(0, count, lower, 0, unroll=4)
 
 
 def prepare_send(strain, pmap, state, ends, mixed, slots, send, spread, flat, srows, load):

time: 86.8 us -> 87.3 us (level)
  no operation moved by 1% of the time
where the time goes in v5:
time: 87.3 us; the launch traced here: 87 us
  Pallas kernels  85.5 us (98%)
  between operations  1.45 us (2%)
    pallas_call x1, Pallas kernels, on_device(): pl.pallas_call(step_kernel, out_shape=(jax.ShapeDtypeStruct((N_DEV, 16, 1...  78.1 us
    pallas_call x1, Pallas kernels, on_device(): pl.pallas_call(unpack_kernel, out_shape=(nodal, nodal, nodal, jax.ShapeDt...  7.42 us

profile of v5, /device:TPU:1, one launch (start us, length us, event | category | flops | bytes accessed | tf_op | source)
XLA Modules:
  0.0 87.0 jit_solution(14260637134913879903)
XLA Ops:
  1.3 78.1 %step.1 = (bf16[128,16,128]{2,1,0:T(8,128)(2,1)}, bf16[128,48,128]{2,1,0:T(8,128)(2,1)}, f32[3,128]{1,0:T(4,128)}, f32[3,128]{1,0:T(4,128)}, f32[3,128]{1,0:T(4,128)}) custom-call(f32[3,128]{1,0:T(4,128)} %disp.1, f32[3,128]{1,0:T(4,128)} %load_ref.1, s32[4,512]{1,0:T(4,128)} %conn.1, f32[12,512]{1,0:T(8,128)} %grads.1, f32[1,512]{1,0:T(1,128)} %bitcast.16, ...), custom_call_target="tpu_custom_call" | custom-call | tf_op jit(solution)/shard_map/step/pallas_call | solution.py:749
  79.4 7.4 %unpack.1 = (f32[3,128]{1,0:T(4,128)}, f32[3,128]{1,0:T(4,128)}, f32[3,128]{1,0:T(4,128)}, bf16[512,3072]{1,0:T(8,128)(2,1)}) custom-call(f32[3,128]{1,0:T(4,128)} %get-tuple-element.9.residual, f32[3,128]{1,0:T(4,128)} %get-tuple-element.10.product, f32[3,128]{1,0:T(4,128)} %get-tuple-element.11.update, bf16[128,16,128]{2,1,0:T(8,128)(2,1)} %get-tuple-element.12.tail_hbm, ...), custom_call_target="tpu_custom_call" | custom-call | tf_op jit(solution)/shard_map/unpack/pallas_call | solution.py:802
